TPU v7x, 32 devices: a whole 2x2x4 slice. The times are simulated.
32 devices in a mesh: depth: 8 (over z, x), stripe: 4 (over y, core).
Axes of the slice: x: 2, y: 2, z: 4, core: 2. Of those that a mesh axis runs over, the one named last changes fastest.
Arguments:
- object_slices: float32 [8, 2, 1024, 384], P('depth', None, 'stripe'), may hold values from -1 to 1, as said below
- probe_wave: bfloat16 [2, 256, 256], replicated, may hold values from -5 to 5
- amplitudes: bfloat16 [16, 256, 256], P('stripe'), may hold values from 0 to 2
- positions: int32 [16, 2], replicated, may hold values from 0 to 255, as said below
- counts: int32 [4], replicated, may hold values from 1 to 4, as said below
Outputs:
- grad_object: float32 [8, 2, 1024, 384], P('depth', None, 'stripe')
Inputs may be any that keep to these rules, and one draw needn't show every extreme that they name: `object_slices`: every cell has magnitude at most 1. `positions`: row offsets lie in 0 to 255 and column offsets in 0 to 128. The counts sum to 8 and the largest equals 4; a stripe's live slots are its first ones.
All inputs are finite; a program needn't handle non-finite values.
Results may differ from a plain program's by a relative error of at most 0.0003.
Values may be sent and summed in bfloat16 or wider, within the bound.
A program may use at most 64 MiB of HBM per device.

v0:
```python
import math

import jax
import jax.numpy as jnp
from jax import lax
from jax.sharding import PartitionSpec as P

smoothing = 0.25
highest = lax.Precision.HIGHEST


def passed_along(block, axis, distance):
    devices = range(lax.axis_size(axis))
    route = [(i - distance, i) for i in devices if i - distance in devices]
    return lax.ppermute(block, axis, route)


def make_tables(length):
    index_row = jnp.arange(length, dtype=jnp.int32)
    product = index_row[:, None] * index_row[None, :] % length
    angle = 2.0 * math.pi * product.astype(jnp.float32) / length
    scale = 1.0 / math.sqrt(length)
    cos_part = jnp.cos(angle) * scale
    sin_part = -jnp.sin(angle) * scale
    neg_part = jnp.sin(angle) * scale
    right_fwd = jnp.concatenate([cos_part, sin_part], axis=1)
    left_fwd = jnp.concatenate([cos_part, sin_part], axis=0)
    right_inv = jnp.concatenate([cos_part, neg_part], axis=1)
    left_inv = jnp.concatenate([cos_part, neg_part], axis=0)
    freq = ((index_row + length // 2) % length - length // 2).astype(jnp.float32)
    phase = (
        -math.pi * (freq[:, None] * freq[:, None] + freq[None, :] * freq[None, :]) / (2.0 * length)
    )
    return (right_fwd, left_fwd, right_inv, left_inv, jnp.cos(phase), jnp.sin(phase))


def transform(real_in, imag_in, right_tab, left_tab):
    length = real_in.shape[0]
    stacked = jnp.concatenate([real_in, imag_in], axis=0)
    first_pass = jnp.dot(stacked, right_tab, precision=highest, preferred_element_type=jnp.float32)
    mid_real = first_pass[:length, :length] - first_pass[length:, length:]
    mid_imag = first_pass[:length, length:] + first_pass[length:, :length]
    second = jnp.dot(
        left_tab,
        jnp.concatenate([mid_real, mid_imag], axis=1),
        precision=highest,
        preferred_element_type=jnp.float32,
    )
    out_real = second[:length, :length] - second[length:, length:]
    out_imag = second[:length, length:] + second[length:, :length]
    return (out_real, out_imag)


def transmit(wave_in, window):
    real_t = wave_in[0] * window[0] - wave_in[1] * window[1]
    imag_t = wave_in[0] * window[1] + wave_in[1] * window[0]
    return (real_t, imag_t)


def advance(wave_in, window, tables):
    right_fwd, left_fwd, right_inv, left_inv, prop_cos, prop_sin = tables
    real_t, imag_t = transmit(wave_in, window)
    spec_real, spec_imag = transform(real_t, imag_t, right_fwd, left_fwd)
    prop_real = spec_real * prop_cos - spec_imag * prop_sin
    prop_imag = spec_real * prop_sin + spec_imag * prop_cos
    out_real, out_imag = transform(prop_real, prop_imag, right_inv, left_inv)
    return jnp.stack([out_real, out_imag])


def exit_adjoint(wave_in, window, amplitude, tables):
    right_fwd, left_fwd = (tables[0], tables[1])
    real_t, imag_t = transmit(wave_in, window)
    far_real, far_imag = transform(real_t, imag_t, right_fwd, left_fwd)
    smooth = jnp.sqrt(far_real * far_real + far_imag * far_imag + smoothing)
    factor = 1.0 - amplitude.astype(jnp.float32) / smooth
    return jnp.stack([factor * far_real, factor * far_imag])


def unfold(adjoint, tables):
    out_real, out_imag = transform(adjoint[0], adjoint[1], tables[2], tables[3])
    return jnp.stack([out_real, out_imag])


def retreat(adjoint, tables):
    right_fwd, left_fwd, right_inv, left_inv, prop_cos, prop_sin = tables
    spec_real, spec_imag = transform(adjoint[0], adjoint[1], right_fwd, left_fwd)
    back_real = spec_real * prop_cos + spec_imag * prop_sin
    back_imag = spec_imag * prop_cos - spec_real * prop_sin
    out_real, out_imag = transform(back_real, back_imag, right_inv, left_inv)
    return jnp.stack([out_real, out_imag])


def slice_grad(wave_in, middle):
    return jnp.stack(
        [
            wave_in[0] * middle[0] + wave_in[1] * middle[1],
            wave_in[0] * middle[1] - wave_in[1] * middle[0],
        ]
    )


def back_wave(window, middle):
    return jnp.stack(
        [
            window[0] * middle[0] + window[1] * middle[1],
            window[0] * middle[1] - window[1] * middle[0],
        ]
    )


def depth_chain(
    object_slab, probe_float, patterns, pattern_index, row_start, col_start, live_mask, tables
):
    depth_count = lax.axis_size("depth")
    depth_index = lax.axis_index("depth")
    slot_count = row_start.shape[0]
    layers = object_slab.shape[0]
    window_size = probe_float.shape[1]
    is_last = depth_index == depth_count - 1
    is_first = depth_index == 0
    step_count = slot_count + depth_count - 1
    empty_wave = jnp.zeros((2, window_size, window_size), jnp.float32)
    stored_start = jnp.zeros((slot_count, layers, 2, window_size, window_size), jnp.float32)
    starts_start = jnp.zeros((slot_count, 2, window_size, window_size), jnp.float32)
    zero_index = jnp.zeros((), jnp.int32)

    def corner_of(layer_id, slot_id):
        return (jnp.int32(layer_id), zero_index, row_start[slot_id], col_start[slot_id])

    def window_at(layer_id, slot_id):
        return lax.dynamic_slice(
            object_slab, corner_of(layer_id, slot_id), (1, 2, window_size, window_size)
        )[0]

    def forward_step(carry, step_id):
        outgoing, stored, starts = carry
        received = passed_along(outgoing, "depth", 1)
        slot_raw = step_id - depth_index
        inside = (slot_raw >= 0) & (slot_raw < slot_count)
        slot_id = jnp.clip(slot_raw, 0, slot_count - 1)
        active = inside & live_mask[slot_id]

        def forward_compute_step(buffers):
            stored, starts = buffers
            wave_in = jnp.where(is_first, probe_float, received)
            stored = lax.dynamic_update_slice(
                stored,
                wave_in[None, None],
                (slot_id, jnp.int32(0), zero_index, zero_index, zero_index),
            )
            window = window_at(0, slot_id)
            pattern = lax.dynamic_index_in_dim(patterns, pattern_index[slot_id], 0, keepdims=False)
            wave_in = lax.cond(
                is_last,
                lambda: exit_adjoint(wave_in, window, pattern, tables),
                lambda: advance(wave_in, window, tables),
            )
            starts = lax.dynamic_update_slice(
                starts, wave_in[None], (slot_id, zero_index, zero_index, zero_index)
            )
            return (wave_in, stored, starts)

        def forward_skip_step(buffers):
            return (empty_wave, buffers[0], buffers[1])

        outgoing, stored, starts = lax.cond(
            active, forward_compute_step, forward_skip_step, (stored, starts)
        )
        return ((outgoing, stored, starts), None)

    (_, stored, starts), _ = lax.scan(
        forward_step,
        (empty_wave, stored_start, starts_start),
        jnp.arange(step_count, dtype=jnp.int32),
    )

    def backward_step(carry, step_id):
        outgoing, gradient = carry
        received = passed_along(outgoing, "depth", -1)
        slot_raw = step_id - (depth_count - 1 - depth_index)
        inside = (slot_raw >= 0) & (slot_raw < slot_count)
        slot_id = jnp.clip(slot_raw, 0, slot_count - 1)
        active = inside & live_mask[slot_id]

        def backward_compute_step(gradient):
            adjoint = jnp.where(is_last, starts[slot_id], received)
            for layer_id in reversed(range(layers)):
                window = window_at(layer_id, slot_id)
                wave_in = stored[slot_id, layer_id]
                middle = lax.cond(
                    is_last, lambda: unfold(adjoint, tables), lambda: retreat(adjoint, tables)
                )
                corner = corner_of(layer_id, slot_id)
                region = lax.dynamic_slice(gradient, corner, (1, 2, window_size, window_size))
                gradient = lax.dynamic_update_slice(
                    gradient, region + slice_grad(wave_in, middle)[None], corner
                )
                adjoint = back_wave(window, middle)
            return (adjoint, gradient)

        def backward_skip_step(gradient):
            return (empty_wave, gradient)

        outgoing, gradient = lax.cond(active, backward_compute_step, backward_skip_step, gradient)
        return ((outgoing, gradient), None)

    grad_start = jnp.zeros(object_slab.shape, jnp.float32)
    (_, gradient), _ = lax.scan(
        backward_step, (empty_wave, grad_start), jnp.arange(step_count, dtype=jnp.int32)
    )
    return gradient


def body(object_slices, probe_wave, amplitudes, positions, counts):
    stripe_index = lax.axis_index("stripe")
    stripe_count = lax.axis_size("stripe")
    stripe_rows = object_slices.shape[2]
    window_size = probe_wave.shape[1]
    capacity = amplitudes.shape[0]
    tables = make_tables(window_size)
    probe_float = probe_wave.astype(jnp.float32)
    whole_slab = lax.all_gather(object_slices, "stripe", axis=2, tiled=True)
    patterns = lax.all_gather(amplitudes, "stripe", axis=0, tiled=True)
    object_slab = jnp.concatenate([whole_slab, whole_slab[:, :, :window_size]], axis=2)
    slot_count = capacity // 2
    offsets = jnp.cumsum(counts) - counts
    global_slot = stripe_index * slot_count + jnp.arange(slot_count, dtype=jnp.int32)
    owner_id = jnp.sum((offsets[None, :] <= global_slot[:, None]).astype(jnp.int32), axis=1) - 1
    onehot = (jnp.arange(stripe_count, dtype=jnp.int32)[None, :] == owner_id[:, None]).astype(
        jnp.int32
    )
    within = global_slot - jnp.sum(onehot * offsets[None, :], axis=1)
    pattern_index = owner_id * capacity + within
    chosen = jnp.take(positions, pattern_index, axis=0)
    row_start = owner_id * stripe_rows + chosen[:, 0]
    col_start = chosen[:, 1]
    live_mask = jnp.ones((slot_count,), jnp.bool_)
    gradient = depth_chain(
        object_slab, probe_float, patterns, pattern_index, row_start, col_start, live_mask, tables
    )
    total_rows = whole_slab.shape[2]
    head_rows = gradient[:, :, :window_size] + gradient[:, :, total_rows:]
    full_grad = jnp.concatenate([head_rows, gradient[:, :, window_size:total_rows]], axis=2)
    return lax.psum_scatter(full_grad, "stripe", scatter_dimension=2, tiled=True)


def solution(mesh):
    return jax.shard_map(
        body,
        mesh=mesh,
        in_specs=(P("depth", None, "stripe", None), P(), P("stripe", None, None), P(), P()),
        out_specs=P("depth", None, "stripe", None),
        check_vma=False,
    )
```

profile of v0, /device:TPU:0, one launch (start us, length us, event | category | flops | bytes accessed | tf_op | source)
XLA Modules:
  0.0 756.4 jit_solution(550692017945356579)
XLA Ops:
  17.2 17.0 %all-gather.5.cloned.1.call-done = bf16[16,256,256]{2,1,0:T(8,128)(2,1)} async-done(((bf16[4,256,256]{2,1,0:T(8,128)(2,1)}), bf16[16,256,256]{2,1,0:T(8,128)(2,1)}) %all-gather.5.cloned.1.call-update) | async-done | bytes 2097168 | tf_op jit(solution)/shard_map/all_gather | solution.py:223
  38.1 26.2 %all-gather.3.cloned.1.call-done = f32[1,2,1024,384]{2,3,1,0:T(8,128)} async-done(((f32[1,2,256,384]{2,3,1,0:T(8,128)}), f32[1,2,1024,384]{2,3,1,0:T(8,128)}) %all-gather.3.cloned.1.call-update) | async-done | bytes 3145744 | tf_op jit(solution)/shard_map/all_gather | solution.py:222
  78.1 224.4 %while.37 = (s32[]{:T(128)}, f32[2,256,256]{1,2,0:T(8,128)}, f32[2,1,2,256,256]{4,3,2,1,0:T(8,128)}, f32[2,2,256,256]{2,3,1,0:T(8,128)}, s32[9]{0:T(128)S(1)}, /...) while((s32[]{:T(128)}, f32[2,256,256]{1,2,0:T(8,128)}, ...), condition=%wide.region_8.9_spmd.clone.clone.clone, body=%wide.region_3.8_spmd.clone.clone.clone.sunk | while | flops 3223584768 | bytes 31198504 | solution.py:171
  84.9 9.5 %collective-permute-done = f32[2,256,256]{2,1,0:T(8,128)S(1)} collective-permute-done((f32[2,256,256]{2,1,0:T(8,128)S(1)}, f32[2,256,256]{2,1,0:T(8,128)S(1)}, u32[]{:S(2)}, u32[]{:S(2)}) %collective-permute-start) | collective-permute-done | bytes 524320 | tf_op jit(solution)/shard_map/while/body/eval_jaxpr/ppermute | solution.py:15
  94.3 19.0 %conditional.14 = (f32[2,256,256]{1,2,0:T(8,128)}, f32[2,1,2,256,256]{4,3,2,1,0:T(8,128)}, f32[2,2,256,256]{2,3,1,0:T(8,128)}) conditional(s32[]{:T(128)} %convert_element_type.103, (f32[2,1,2,256,256]{4,3,2,1,0:T(8,128)}, f32[2,2,256,256]{2,3,1,0:T(8,128)}) %tuple.165, (pred[]{:T(512)}, pred[]{:T(512)}, f32[2,256,256]{2,1,0:T(8,128)}, ...), branch_computations={%region_4.4_spmd, %region_5.7_spmd.clone} | conditional | flops 3223453696 | bytes 27789160 | solution.py:166
  117.9 9.0 %collective-permute-done = f32[2,256,256]{2,1,0:T(8,128)S(1)} collective-permute-done((f32[2,256,256]{2,1,0:T(8,128)S(1)}, f32[2,256,256]{2,1,0:T(8,128)S(1)}, u32[]{:S(2)}, u32[]{:S(2)}) %collective-permute-start) | collective-permute-done | bytes 524320 | tf_op jit(solution)/shard_map/while/body/eval_jaxpr/ppermute | solution.py:15
  126.9 19.1 %conditional.14 = (f32[2,256,256]{1,2,0:T(8,128)}, f32[2,1,2,256,256]{4,3,2,1,0:T(8,128)}, f32[2,2,256,256]{2,3,1,0:T(8,128)}) conditional(s32[]{:T(128)} %convert_element_type.103, (f32[2,1,2,256,256]{4,3,2,1,0:T(8,128)}, f32[2,2,256,256]{2,3,1,0:T(8,128)}) %tuple.165, (pred[]{:T(512)}, pred[]{:T(512)}, f32[2,256,256]{2,1,0:T(8,128)}, ...), branch_computations={%region_4.4_spmd, %region_5.7_spmd.clone} | conditional | flops 3223453696 | bytes 27789160 | solution.py:166
  153.6 8.2 %collective-permute-done = f32[2,256,256]{2,1,0:T(8,128)S(1)} collective-permute-done((f32[2,256,256]{2,1,0:T(8,128)S(1)}, f32[2,256,256]{2,1,0:T(8,128)S(1)}, u32[]{:S(2)}, u32[]{:S(2)}) %collective-permute-start) | collective-permute-done | bytes 524320 | tf_op jit(solution)/shard_map/while/body/eval_jaxpr/ppermute | solution.py:15
  163.9 22.7 %collective-permute-start = (f32[2,256,256]{2,1,0:T(8,128)S(1)}, f32[2,256,256]{2,1,0:T(8,128)S(1)}, u32[]{:S(2)}, u32[]{:S(2)}) collective-permute-start(f32[2,256,256]{2,1,0:T(8,128)S(1)} %copy.52), channel_id=1, source_target_pairs={{0,4},{4,8},{8,12},{12,16},{16,20},{20,24},{24,28},{1,5},{5,9},{9,... | collective-permute-start | bytes 1572872 | tf_op jit(solution)/shard_map/while/body/eval_jaxpr/ppermute | solution.py:15
  213.1 22.9 %collective-permute-start = (f32[2,256,256]{2,1,0:T(8,128)S(1)}, f32[2,256,256]{2,1,0:T(8,128)S(1)}, u32[]{:S(2)}, u32[]{:S(2)}) collective-permute-start(f32[2,256,256]{2,1,0:T(8,128)S(1)} %copy.52), channel_id=1, source_target_pairs={{0,4},{4,8},{8,12},{12,16},{16,20},{20,24},{24,28},{1,5},{5,9},{9,... | collective-permute-start | bytes 1572872 | tf_op jit(solution)/shard_map/while/body/eval_jaxpr/ppermute | solution.py:15
  260.8 20.2 %collective-permute-start = (f32[2,256,256]{2,1,0:T(8,128)S(1)}, f32[2,256,256]{2,1,0:T(8,128)S(1)}, u32[]{:S(2)}, u32[]{:S(2)}) collective-permute-start(f32[2,256,256]{2,1,0:T(8,128)S(1)} %copy.52), channel_id=1, source_target_pairs={{0,4},{4,8},{8,12},{12,16},{16,20},{20,24},{24,28},{1,5},{5,9},{9,... | collective-permute-start | bytes 1572872 | tf_op jit(solution)/shard_map/while/body/eval_jaxpr/ppermute | solution.py:15
  310.6 394.4 %while.38 = (s32[]{:T(128)}, f32[2,256,256]{1,2,0:T(8,128)}, f32[1,2,1280,384]{2,3,1,0:T(8,128)}, s32[9]{0:T(128)S(1)}, s32[]{:T(128)}, /*index=5*/s32[2]{0:T(12...) while((s32[]{:T(128)}, f32[2,256,256]{1,2,0:T(8,128)}, ...), condition=%wide.region_14.15_spmd.clone.clone.clone, body=%wide.region_9.14_spmd.clone.clone.clone.sunk | while | flops 3224109056 | bytes 29623972 | solution.py:208
  314.5 26.5 %collective-permute-done.1 = f32[2,256,256]{2,1,0:T(8,128)S(1)} collective-permute-done((f32[2,256,256]{2,1,0:T(8,128)S(1)}, f32[2,256,256]{2,1,0:T(8,128)S(1)}, u32[]{:S(2)}, u32[]{:S(2)}) %collective-permute-start.1) | collective-permute-done | bytes 524320 | tf_op jit(solution)/shard_map/while/body/eval_jaxpr/ppermute | solution.py:15
  345.7 9.8 %collective-permute-done.1 = f32[2,256,256]{2,1,0:T(8,128)S(1)} collective-permute-done((f32[2,256,256]{2,1,0:T(8,128)S(1)}, f32[2,256,256]{2,1,0:T(8,128)S(1)}, u32[]{:S(2)}, u32[]{:S(2)}) %collective-permute-start.1) | collective-permute-done | bytes 524320 | tf_op jit(solution)/shard_map/while/body/eval_jaxpr/ppermute | solution.py:15
  360.2 24.6 %collective-permute-done.1 = f32[2,256,256]{2,1,0:T(8,128)S(1)} collective-permute-done((f32[2,256,256]{2,1,0:T(8,128)S(1)}, f32[2,256,256]{2,1,0:T(8,128)S(1)}, u32[]{:S(2)}, u32[]{:S(2)}) %collective-permute-start.1) | collective-permute-done | bytes 524320 | tf_op jit(solution)/shard_map/while/body/eval_jaxpr/ppermute | solution.py:15
  389.6 9.5 %collective-permute-done.1 = f32[2,256,256]{2,1,0:T(8,128)S(1)} collective-permute-done((f32[2,256,256]{2,1,0:T(8,128)S(1)}, f32[2,256,256]{2,1,0:T(8,128)S(1)}, u32[]{:S(2)}, u32[]{:S(2)}) %collective-permute-start.1) | collective-permute-done | bytes 524320 | tf_op jit(solution)/shard_map/while/body/eval_jaxpr/ppermute | solution.py:15
  403.8 27.7 %collective-permute-done.1 = f32[2,256,256]{2,1,0:T(8,128)S(1)} collective-permute-done((f32[2,256,256]{2,1,0:T(8,128)S(1)}, f32[2,256,256]{2,1,0:T(8,128)S(1)}, u32[]{:S(2)}, u32[]{:S(2)}) %collective-permute-start.1) | collective-permute-done | bytes 524320 | tf_op jit(solution)/shard_map/while/body/eval_jaxpr/ppermute | solution.py:15
  436.2 8.4 %collective-permute-done.1 = f32[2,256,256]{2,1,0:T(8,128)S(1)} collective-permute-done((f32[2,256,256]{2,1,0:T(8,128)S(1)}, f32[2,256,256]{2,1,0:T(8,128)S(1)}, u32[]{:S(2)}, u32[]{:S(2)}) %collective-permute-start.1) | collective-permute-done | bytes 524320 | tf_op jit(solution)/shard_map/while/body/eval_jaxpr/ppermute | solution.py:15
  449.4 24.8 %collective-permute-done.1 = f32[2,256,256]{2,1,0:T(8,128)S(1)} collective-permute-done((f32[2,256,256]{2,1,0:T(8,128)S(1)}, f32[2,256,256]{2,1,0:T(8,128)S(1)}, u32[]{:S(2)}, u32[]{:S(2)}) %collective-permute-start.1) | collective-permute-done | bytes 524320 | tf_op jit(solution)/shard_map/while/body/eval_jaxpr/ppermute | solution.py:15
  478.9 163.4 %collective-permute-done.1 = f32[2,256,256]{2,1,0:T(8,128)S(1)} collective-permute-done((f32[2,256,256]{2,1,0:T(8,128)S(1)}, f32[2,256,256]{2,1,0:T(8,128)S(1)}, u32[]{:S(2)}, u32[]{:S(2)}) %collective-permute-start.1) | collective-permute-done | bytes 524320 | tf_op jit(solution)/shard_map/while/body/eval_jaxpr/ppermute | solution.py:15
  642.3 23.2 %conditional.15 = (f32[2,256,256]{1,2,0:T(8,128)}, f32[1,2,1280,384]{2,3,1,0:T(8,128)}) conditional(s32[]{:T(128)} %convert_element_type.104, f32[1,2,1280,384]{2,3,1,0:T(8,128)} %get-tuple-element.1530, (s32[]{:T(128)}, s32[2]{0:T(128)S(1)}, s32[2]{0:T(128)S(1)}, f32[1,2,1280,384]{2,3,1,0:T(8,128)}, pred[]{:T(512)}, ...), branch_computations={%region_10.10_spmd, %region_11.13_spmd.clone} | conditional | flops 3223977984 | bytes 26214692 | solution.py:204
  669.4 11.3 %collective-permute-done.1 = f32[2,256,256]{2,1,0:T(8,128)S(1)} collective-permute-done((f32[2,256,256]{2,1,0:T(8,128)S(1)}, f32[2,256,256]{2,1,0:T(8,128)S(1)}, u32[]{:S(2)}, u32[]{:S(2)}) %collective-permute-start.1) | collective-permute-done | bytes 524320 | tf_op jit(solution)/shard_map/while/body/eval_jaxpr/ppermute | solution.py:15
  680.7 24.3 %conditional.15 = (f32[2,256,256]{1,2,0:T(8,128)}, f32[1,2,1280,384]{2,3,1,0:T(8,128)}) conditional(s32[]{:T(128)} %convert_element_type.104, f32[1,2,1280,384]{2,3,1,0:T(8,128)} %get-tuple-element.1530, (s32[]{:T(128)}, s32[2]{0:T(128)S(1)}, s32[2]{0:T(128)S(1)}, f32[1,2,1280,384]{2,3,1,0:T(8,128)}, pred[]{:T(512)}, ...), branch_computations={%region_10.10_spmd, %region_11.13_spmd.clone} | conditional | flops 3223977984 | bytes 26214692 | solution.py:204
  715.3 34.6 %reduce-scatter.2.cloned.1.call-done = f32[1,2,256,384]{3,2,1,0:T(8,128)} async-done(((f32[1,2,1024,384]{3,2,1,0:T(8,128)}), f32[1,2,256,384]{3,2,1,0:T(8,128)}) %reduce-scatter.2.cloned.1.call-update) | async-done | bytes 786448 | tf_op jit(solution)/shard_map/reduce_scatter | solution.py:244
  (234 shorter events, 272.0 us)
Async XLA Ops:
  6.5 27.7 %all-gather.5.cloned.1.call-start = ((), (), s32[]{:S(2)}) async-start(), calls=%async_computation.2 | async-start | bytes 2621440 | tf_op jit(solution)/shard_map/all_gather | solution.py:223
  7.3 57.1 %all-gather.3.cloned.1.call-start = ((), (), s32[]{:S(2)}) async-start(), calls=%async_computation.1 | async-start | bytes 3932160 | tf_op jit(solution)/shard_map/all_gather | solution.py:222
  9.6 740.2 %reduce-scatter.2.cloned.1.call-start = ((), (), s32[]{:S(2)}) async-start(), calls=%async_computation.3 | async-start | bytes 3932160 | tf_op jit(solution)/shard_map/reduce_scatter | solution.py:244
  79.4 14.9 %collective-permute-start = (f32[2,256,256]{2,1,0:T(8,128)S(1)}, f32[2,256,256]{2,1,0:T(8,128)S(1)}, u32[]{:S(2)}, u32[]{:S(2)}) collective-permute-start(f32[2,256,256]{2,1,0:T(8,128)S(1)} %copy.52), channel_id=1, source_target_pairs={{0,4},{4,8},{8,12},{12,16},{16,20},{20,24},{24,28},{1,5},{5,9},{9,... | collective-permute-start | bytes 1572872 | tf_op jit(solution)/shard_map/while/body/eval_jaxpr/ppermute | solution.py:15
  94.3 6.4 copy-start.2
  114.5 12.4 %collective-permute-start = (f32[2,256,256]{2,1,0:T(8,128)S(1)}, f32[2,256,256]{2,1,0:T(8,128)S(1)}, u32[]{:S(2)}, u32[]{:S(2)}) collective-permute-start(f32[2,256,256]{2,1,0:T(8,128)S(1)} %copy.52), channel_id=1, source_target_pairs={{0,4},{4,8},{8,12},{12,16},{16,20},{20,24},{24,28},{1,5},{5,9},{9,... | collective-permute-start | bytes 1572872 | tf_op jit(solution)/shard_map/while/body/eval_jaxpr/ppermute | solution.py:15
  126.9 6.4 copy-start.2
  147.2 14.6 %collective-permute-start = (f32[2,256,256]{2,1,0:T(8,128)S(1)}, f32[2,256,256]{2,1,0:T(8,128)S(1)}, u32[]{:S(2)}, u32[]{:S(2)}) collective-permute-start(f32[2,256,256]{2,1,0:T(8,128)S(1)} %copy.52), channel_id=1, source_target_pairs={{0,4},{4,8},{8,12},{12,16},{16,20},{20,24},{24,28},{1,5},{5,9},{9,... | collective-permute-start | bytes 1572872 | tf_op jit(solution)/shard_map/while/body/eval_jaxpr/ppermute | solution.py:15
  163.9 32.1 %collective-permute-start = (f32[2,256,256]{2,1,0:T(8,128)S(1)}, f32[2,256,256]{2,1,0:T(8,128)S(1)}, u32[]{:S(2)}, u32[]{:S(2)}) collective-permute-start(f32[2,256,256]{2,1,0:T(8,128)S(1)} %copy.52), channel_id=1, source_target_pairs={{0,4},{4,8},{8,12},{12,16},{16,20},{20,24},{24,28},{1,5},{5,9},{9,... | collective-permute-start | bytes 1572872 | tf_op jit(solution)/shard_map/while/body/eval_jaxpr/ppermute | solution.py:15
  198.1 13.0 %collective-permute-start = (f32[2,256,256]{2,1,0:T(8,128)S(1)}, f32[2,256,256]{2,1,0:T(8,128)S(1)}, u32[]{:S(2)}, u32[]{:S(2)}) collective-permute-start(f32[2,256,256]{2,1,0:T(8,128)S(1)} %copy.52), channel_id=1, source_target_pairs={{0,4},{4,8},{8,12},{12,16},{16,20},{20,24},{24,28},{1,5},{5,9},{9,... | collective-permute-start | bytes 1572872 | tf_op jit(solution)/shard_map/while/body/eval_jaxpr/ppermute | solution.py:15
  213.1 31.0 %collective-permute-start = (f32[2,256,256]{2,1,0:T(8,128)S(1)}, f32[2,256,256]{2,1,0:T(8,128)S(1)}, u32[]{:S(2)}, u32[]{:S(2)}) collective-permute-start(f32[2,256,256]{2,1,0:T(8,128)S(1)} %copy.52), channel_id=1, source_target_pairs={{0,4},{4,8},{8,12},{12,16},{16,20},{20,24},{24,28},{1,5},{5,9},{9,... | collective-permute-start | bytes 1572872 | tf_op jit(solution)/shard_map/while/body/eval_jaxpr/ppermute | solution.py:15
  246.2 12.5 %collective-permute-start = (f32[2,256,256]{2,1,0:T(8,128)S(1)}, f32[2,256,256]{2,1,0:T(8,128)S(1)}, u32[]{:S(2)}, u32[]{:S(2)}) collective-permute-start(f32[2,256,256]{2,1,0:T(8,128)S(1)} %copy.52), channel_id=1, source_target_pairs={{0,4},{4,8},{8,12},{12,16},{16,20},{20,24},{24,28},{1,5},{5,9},{9,... | collective-permute-start | bytes 1572872 | tf_op jit(solution)/shard_map/while/body/eval_jaxpr/ppermute | solution.py:15
  260.8 26.8 %collective-permute-start = (f32[2,256,256]{2,1,0:T(8,128)S(1)}, f32[2,256,256]{2,1,0:T(8,128)S(1)}, u32[]{:S(2)}, u32[]{:S(2)}) collective-permute-start(f32[2,256,256]{2,1,0:T(8,128)S(1)} %copy.52), channel_id=1, source_target_pairs={{0,4},{4,8},{8,12},{12,16},{16,20},{20,24},{24,28},{1,5},{5,9},{9,... | collective-permute-start | bytes 1572872 | tf_op jit(solution)/shard_map/while/body/eval_jaxpr/ppermute | solution.py:15
  289.7 12.0 %collective-permute-start = (f32[2,256,256]{2,1,0:T(8,128)S(1)}, f32[2,256,256]{2,1,0:T(8,128)S(1)}, u32[]{:S(2)}, u32[]{:S(2)}) collective-permute-start(f32[2,256,256]{2,1,0:T(8,128)S(1)} %copy.52), channel_id=1, source_target_pairs={{0,4},{4,8},{8,12},{12,16},{16,20},{20,24},{24,28},{1,5},{5,9},{9,... | collective-permute-start | bytes 1572872 | tf_op jit(solution)/shard_map/while/body/eval_jaxpr/ppermute | solution.py:15
  311.8 29.1 %collective-permute-start.1 = (f32[2,256,256]{2,1,0:T(8,128)S(1)}, f32[2,256,256]{2,1,0:T(8,128)S(1)}, u32[]{:S(2)}, u32[]{:S(2)}) collective-permute-start(f32[2,256,256]{2,1,0:T(8,128)S(1)} %copy.53), channel_id=1, source_target_pairs={{4,0},{8,4},{12,8},{16,12},{20,16},{24,20},{28,24},{5,1},{9,5},{13... | collective-permute-start | bytes 1572872 | tf_op jit(solution)/shard_map/while/body/eval_jaxpr/ppermute | solution.py:15
  343.1 12.4 %collective-permute-start.1 = (f32[2,256,256]{2,1,0:T(8,128)S(1)}, f32[2,256,256]{2,1,0:T(8,128)S(1)}, u32[]{:S(2)}, u32[]{:S(2)}) collective-permute-start(f32[2,256,256]{2,1,0:T(8,128)S(1)} %copy.53), channel_id=1, source_target_pairs={{4,0},{8,4},{12,8},{16,12},{20,16},{24,20},{28,24},{5,1},{9,5},{13... | collective-permute-start | bytes 1572872 | tf_op jit(solution)/shard_map/while/body/eval_jaxpr/ppermute | solution.py:15
  357.6 27.3 %collective-permute-start.1 = (f32[2,256,256]{2,1,0:T(8,128)S(1)}, f32[2,256,256]{2,1,0:T(8,128)S(1)}, u32[]{:S(2)}, u32[]{:S(2)}) collective-permute-start(f32[2,256,256]{2,1,0:T(8,128)S(1)} %copy.53), channel_id=1, source_target_pairs={{4,0},{8,4},{12,8},{16,12},{20,16},{24,20},{28,24},{5,1},{9,5},{13... | collective-permute-start | bytes 1572872 | tf_op jit(solution)/shard_map/while/body/eval_jaxpr/ppermute | solution.py:15
  387.0 12.1 %collective-permute-start.1 = (f32[2,256,256]{2,1,0:T(8,128)S(1)}, f32[2,256,256]{2,1,0:T(8,128)S(1)}, u32[]{:S(2)}, u32[]{:S(2)}) collective-permute-start(f32[2,256,256]{2,1,0:T(8,128)S(1)} %copy.53), channel_id=1, source_target_pairs={{4,0},{8,4},{12,8},{16,12},{20,16},{24,20},{28,24},{5,1},{9,5},{13... | collective-permute-start | bytes 1572872 | tf_op jit(solution)/shard_map/while/body/eval_jaxpr/ppermute | solution.py:15
  401.1 30.3 %collective-permute-start.1 = (f32[2,256,256]{2,1,0:T(8,128)S(1)}, f32[2,256,256]{2,1,0:T(8,128)S(1)}, u32[]{:S(2)}, u32[]{:S(2)}) collective-permute-start(f32[2,256,256]{2,1,0:T(8,128)S(1)} %copy.53), channel_id=1, source_target_pairs={{4,0},{8,4},{12,8},{16,12},{20,16},{24,20},{28,24},{5,1},{9,5},{13... | collective-permute-start | bytes 1572872 | tf_op jit(solution)/shard_map/while/body/eval_jaxpr/ppermute | solution.py:15
  433.6 11.1 %collective-permute-start.1 = (f32[2,256,256]{2,1,0:T(8,128)S(1)}, f32[2,256,256]{2,1,0:T(8,128)S(1)}, u32[]{:S(2)}, u32[]{:S(2)}) collective-permute-start(f32[2,256,256]{2,1,0:T(8,128)S(1)} %copy.53), channel_id=1, source_target_pairs={{4,0},{8,4},{12,8},{16,12},{20,16},{24,20},{28,24},{5,1},{9,5},{13... | collective-permute-start | bytes 1572872 | tf_op jit(solution)/shard_map/while/body/eval_jaxpr/ppermute | solution.py:15
  446.7 27.5 %collective-permute-start.1 = (f32[2,256,256]{2,1,0:T(8,128)S(1)}, f32[2,256,256]{2,1,0:T(8,128)S(1)}, u32[]{:S(2)}, u32[]{:S(2)}) collective-permute-start(f32[2,256,256]{2,1,0:T(8,128)S(1)} %copy.53), channel_id=1, source_target_pairs={{4,0},{8,4},{12,8},{16,12},{20,16},{24,20},{28,24},{5,1},{9,5},{13... | collective-permute-start | bytes 1572872 | tf_op jit(solution)/shard_map/while/body/eval_jaxpr/ppermute | solution.py:15
  476.3 166.1 %collective-permute-start.1 = (f32[2,256,256]{2,1,0:T(8,128)S(1)}, f32[2,256,256]{2,1,0:T(8,128)S(1)}, u32[]{:S(2)}, u32[]{:S(2)}) collective-permute-start(f32[2,256,256]{2,1,0:T(8,128)S(1)} %copy.53), channel_id=1, source_target_pairs={{4,0},{8,4},{12,8},{16,12},{20,16},{24,20},{28,24},{5,1},{9,5},{13... | collective-permute-start | bytes 1572872 | tf_op jit(solution)/shard_map/while/body/eval_jaxpr/ppermute | solution.py:15
  666.8 14.0 %collective-permute-start.1 = (f32[2,256,256]{2,1,0:T(8,128)S(1)}, f32[2,256,256]{2,1,0:T(8,128)S(1)}, u32[]{:S(2)}, u32[]{:S(2)}) collective-permute-start(f32[2,256,256]{2,1,0:T(8,128)S(1)} %copy.53), channel_id=1, source_target_pairs={{4,0},{8,4},{12,8},{16,12},{20,16},{24,20},{28,24},{5,1},{9,5},{13... | collective-permute-start | bytes 1572872 | tf_op jit(solution)/shard_map/while/body/eval_jaxpr/ppermute | solution.py:15
  710.5 2.9 slice-start
  (3 other events, 6.6 us)
Sparse Core Ops, SparseCore 0:
  8.9 25.2 all-gather.4
  35.8 28.4 all-gather.2
  715.4 34.4 reduce-scatter.1
where the time goes:
time: 759 us; the launch traced here: 756 us
  waiting for transfers between devices  445 us (59%)
  local copies, waits for them, and re-layouts  112 us (15%)
  starting transfers between devices  102 us (13%)
  other arithmetic  41.1 us (5%)
  loops' own time  26.8 us (4%)
  matrix products  16.8 us (2%)
  between operations  13.2 us (2%)
    ppermute x18, waiting for transfers between devices, passed_along(): return lax.ppermute(block, axis, route)  367 us
    ppermute x18, starting transfers between devices, passed_along(): return lax.ppermute(block, axis, route)  101 us
    reduce_scatter x1, waiting for transfers between devices, body(): lax.psum_scatter(full_grad, 'stripe', scatter_dimension=2, tiled=True)  34.6 us
    all_gather x1, waiting for transfers between devices, body(): whole_slab = lax.all_gather(object_slices, 'stripe', axis=2, tiled=True)  26.2 us
    while x18, local copies, waits for them, and re-layouts  22.2 us
    unnamed x8, local copies, waits for them, and re-layouts  19.7 us
    all_gather x1, waiting for transfers between devices, body(): patterns = lax.all_gather(amplitudes, 'stripe', axis=0, tiled=True)  17 us
  transfers between devices with their start and end apart: 21, of which 21 were waited for; matrix products, arithmetic and copies ran while one was open for 4% of the time, Pallas kernels for 0%

commit v1 on v0

v1 whole, which is shorter than its diff:
```python
import functools

import jax
import jax.numpy as jnp
import numpy as np
from jax import lax
from jax.experimental import pallas as pl
from jax.experimental.pallas import tpu as pltpu
from jax.sharding import PartitionSpec as P

smoothing = 0.25
LEVELS = 32767.0
MESH = pl.DeviceIdType.MESH


def right_form(matrix):
    return np.block([[matrix.real, matrix.imag], [-matrix.imag, matrix.real]])


def make_tables(length):
    half = length // 2
    index = np.arange(length)
    dft = np.exp(-2j * np.pi * (np.outer(index, index) % length) / length) / np.sqrt(length)
    freq = (index + half) % length - half
    fresnel = np.exp(-1j * np.pi * freq.astype(np.float64) ** 2 / (2.0 * length))
    prop = dft.conj() @ (fresnel[:, None] * dft)
    first, second = prop[:half, :half], prop[:half, half:]
    parts = [(first + second) / 2, (first - second) / 2, dft[:half, 0::2], dft[:half, 1::2]]
    tables = []
    for part in parts:
        right = right_form(part)
        tables += [right, right.T]
    stacked = np.stack(tables).astype(np.float32)
    high = stacked.astype(jnp.bfloat16)
    low = (stacked - high.astype(np.float32)).astype(jnp.bfloat16)
    order = np.concatenate([np.arange(0, length, 2), np.arange(1, length, 2)])
    pick = np.zeros((length, length), np.float32)
    pick[np.arange(length), order] = 1.0
    picks = np.stack([pick, pick.T]).astype(jnp.bfloat16)
    return np.concatenate([high, low, picks], axis=0)


def parts_of(value):
    high = value.astype(jnp.bfloat16)
    low = (value - high.astype(jnp.float32)).astype(jnp.bfloat16)
    return high, low


def dot(a, b):
    return jnp.dot(a, b, preferred_element_type=jnp.float32)


def worker_of(slot, stripe, stride):
    return slot * stride + lax.rem(slot + stripe, 2)


def kernel(
    depth_count, capacity, rows_ref, cols_ref, live_ref, win_ref, probe_ref, amp_ref, table_ref,
    own_ref, next_ref,
    wins, waves, gout, gscale, gin, gin_scale, rstack, lstack, adj_buf,
    send_w, recv_w, send_g, recv_g, send_s, recv_s,
):
    me = lax.axis_index("depth")
    stripe = lax.axis_index("stripe")
    stride = depth_count // capacity
    length = win_ref.shape[-1]
    half = length // 2
    count = (table_ref.shape[0] - 2) // 2

    barrier = pltpu.get_barrier_semaphore()

    @pl.loop(1, depth_count)
    def greet(step):
        other = lax.rem(me + step, depth_count)
        pl.semaphore_signal(barrier, inc=1, device_id=(other, stripe), device_id_type=MESH)

    pl.semaphore_wait(barrier, depth_count - 1)

    def window_copy(slot, target):
        return pltpu.make_async_remote_copy(
            src_ref=win_ref.at[slot], dst_ref=wins.at[me], send_sem=send_w.at[slot],
            recv_sem=recv_w.at[me], device_id=(target, stripe), device_id_type=MESH,
        )

    for slot in range(capacity):
        target = worker_of(slot, stripe, stride)

        @pl.when(me != target)
        def _():
            window_copy(slot, target).start()

        @pl.when(me == target)
        def _():
            pltpu.make_async_copy(win_ref.at[slot], wins.at[me], recv_w.at[me]).start()

    my_slot = me // stride
    is_worker = me == worker_of(my_slot, stripe, stride)

    def wait_window(layer):
        pltpu.make_async_copy(win_ref.at[0], wins.at[layer], recv_w.at[layer]).wait()

    def grad_copy(layer):
        return pltpu.make_async_remote_copy(
            src_ref=gout.at[layer], dst_ref=gin.at[my_slot], send_sem=send_g.at[layer],
            recv_sem=recv_g.at[my_slot], device_id=(layer, stripe), device_id_type=MESH,
        )

    def scale_copy(layer):
        return pltpu.make_async_remote_copy(
            src_ref=gscale.at[layer], dst_ref=gin_scale.at[my_slot], send_sem=send_s.at[layer],
            recv_sem=recv_s.at[my_slot], device_id=(layer, stripe), device_id_type=MESH,
        )

    def right_dot(value, which):
        high, low = parts_of(value)
        return dot(jnp.concatenate([high, high, low], axis=1), rstack[which])

    def left_dot(which, value):
        high, low = parts_of(value)
        return dot(lstack[which], jnp.concatenate([high, high, low], axis=0))

    def split_lanes(re, im):
        return (
            jnp.concatenate([re[:, :half] + re[:, half:], im[:, :half] + im[:, half:]], axis=1),
            jnp.concatenate([re[:, :half] - re[:, half:], im[:, :half] - im[:, half:]], axis=1),
        )

    def split_rows(re, im):
        return (
            jnp.concatenate([re[:half] + re[half:], im[:half] + im[half:]], axis=0),
            jnp.concatenate([re[:half] - re[half:], im[:half] - im[half:]], axis=0),
        )

    def join_lanes(p, q):
        return (
            jnp.concatenate([p[:, :half] + q[:, :half], p[:, :half] - q[:, :half]], axis=1),
            jnp.concatenate([p[:, half:] + q[:, half:], p[:, half:] - q[:, half:]], axis=1),
        )

    def join_rows(p, q):
        return (
            jnp.concatenate([p[:half] + q[:half], p[:half] - q[:half]], axis=0),
            jnp.concatenate([p[half:] + q[half:], p[half:] - q[half:]], axis=0),
        )

    def propagate(re, im):
        u, v = split_lanes(re, im)
        re, im = join_lanes(right_dot(u, 0), right_dot(v, 1))
        u, v = split_rows(re, im)
        return join_rows(left_dot(0, u), left_dot(1, v))

    def window_of(layer):
        value = wins[layer].astype(jnp.int32).astype(jnp.float32) * (1.0 / LEVELS)
        return value[0], value[1]

    def emit(layer, re, im):
        for part, value in enumerate((re, im)):
            most = jnp.max(jnp.abs(value), axis=0, keepdims=True)
            most = jnp.maximum(most, 1e-30)
            gout[layer, part] = jnp.round(value * (LEVELS / most)).astype(jnp.int32).astype(jnp.int16)
            gscale[layer, pl.ds(part, 1), :] = most * (1.0 / LEVELS)

        @pl.when(layer != me)
        def _():
            grad_copy(layer).start()
            scale_copy(layer).start()

        @pl.when(layer == me)
        def _():
            pltpu.make_async_copy(gout.at[layer], gin.at[my_slot], recv_g.at[my_slot]).start()
            pltpu.make_async_copy(gscale.at[layer], gin_scale.at[my_slot], recv_s.at[my_slot]).start()

    @pl.when(is_worker)
    def _():
        for which in range(count // 2):
            high, low = table_ref[2 * which], table_ref[count + 2 * which]
            rstack[which] = jnp.concatenate([high, low, high], axis=0)
            high, low = table_ref[2 * which + 1], table_ref[count + 2 * which + 1]
            lstack[which] = jnp.concatenate([high, low, high], axis=1)
        waves[0] = probe_ref[...].astype(jnp.float32)
        gscale[...] = jnp.zeros(gscale.shape, jnp.float32)

        @pl.loop(0, depth_count - 1)
        def forward(layer):
            wait_window(layer)
            win_re, win_im = window_of(layer)
            re, im = waves[layer, 0], waves[layer, 1]
            re, im = propagate(re * win_re - im * win_im, re * win_im + im * win_re)
            waves[layer + 1, 0] = re
            waves[layer + 1, 1] = im

        last = depth_count - 1
        wait_window(last)
        win_re, win_im = window_of(last)
        wave_re, wave_im = waves[last, 0], waves[last, 1]
        re = wave_re * win_re - wave_im * win_im
        im = wave_re * win_im + wave_im * win_re
        u, v = split_lanes(re, im)
        even, odd = right_dot(u, 2), right_dot(v, 3)
        re = jnp.concatenate([even[:, :half], odd[:, :half]], axis=1)
        im = jnp.concatenate([even[:, half:], odd[:, half:]], axis=1)
        u, v = split_rows(re, im)
        even, odd = left_dot(2, u), left_dot(3, v)
        pick_rows, pick_cols = table_ref[2 * count], table_ref[2 * count + 1]
        amp = dot(dot(pick_rows, amp_ref[...]).astype(jnp.bfloat16), pick_cols)
        re = jnp.concatenate([even[:half], odd[:half]], axis=0)
        im = jnp.concatenate([even[half:], odd[half:]], axis=0)
        factor = 1.0 - amp / jnp.sqrt(re * re + im * im + smoothing)
        re, im = factor * re, factor * im
        def left_back(which, value):
            high, low = parts_of(value)
            table = table_ref[2 * which]
            table_low = table_ref[count + 2 * which]
            return dot(table, high) + dot(table_low, high) + dot(table, low)

        def right_back(value, which):
            high, low = parts_of(value)
            table = table_ref[2 * which + 1]
            table_low = table_ref[count + 2 * which + 1]
            return dot(high, table) + dot(high, table_low) + dot(low, table)

        re, im = join_rows(
            left_back(2, jnp.concatenate([re[:half], im[:half]], axis=0)),
            left_back(3, jnp.concatenate([re[half:], im[half:]], axis=0)),
        )
        mid_re, mid_im = join_lanes(
            right_back(jnp.concatenate([re[:, :half], im[:, :half]], axis=1), 2),
            right_back(jnp.concatenate([re[:, half:], im[:, half:]], axis=1), 3),
        )
        emit(
            last,
            wave_re * mid_re + wave_im * mid_im,
            wave_re * mid_im - wave_im * mid_re,
        )
        adj_buf[0] = win_re * mid_re + win_im * mid_im
        adj_buf[1] = win_im * mid_re - win_re * mid_im

        @pl.loop(1, depth_count)
        def backward(step):
            layer = last - step
            mid_re, mid_conj = propagate(adj_buf[0], adj_buf[1])
            win_re, win_im = window_of(layer)
            wave_re, wave_im = waves[layer, 0], waves[layer, 1]
            emit(
                layer,
                wave_re * mid_re - wave_im * mid_conj,
                -(wave_re * mid_conj + wave_im * mid_re),
            )
            adj_buf[0] = win_re * mid_re - win_im * mid_conj
            adj_buf[1] = win_im * mid_re + win_re * mid_conj

    rows = own_ref.shape[1]
    row_index = lax.broadcasted_iota(jnp.int32, (rows, half), 0)
    col_index = lax.broadcasted_iota(jnp.int32, (rows, half), 1)
    own_ref[...] = jnp.zeros(own_ref.shape, jnp.float32)
    next_ref[...] = jnp.zeros(next_ref.shape, jnp.float32)
    for slot in range(capacity):
        pltpu.make_async_copy(gout.at[0], gin.at[slot], recv_g.at[slot]).wait()
        pltpu.make_async_copy(gscale.at[0], gin_scale.at[slot], recv_s.at[slot]).wait()
        row, col, live = rows_ref[slot], cols_ref[slot], live_ref[slot]
        here = row_index >= row
        near = col_index >= col
        for part in range(2):
            value = gin[slot, part].astype(jnp.int32).astype(jnp.float32)
            value = value * gin_scale[slot, pl.ds(part, 1), :]
            value = jnp.where(live > 0, value, 0.0)
            left, mid = value[:, :half], value[:, half:]
            pieces = (jnp.where(near, left, 0.0), mid, jnp.where(near, 0.0, left))
            for place, piece in enumerate(pieces):
                lanes = pl.ds(place * half, half)
                own_ref[part, :, lanes] += jnp.where(here, piece, 0.0)
                next_ref[part, :, lanes] += jnp.where(here, 0.0, piece)

    for slot in range(capacity):
        target = worker_of(slot, stripe, stride)

        @pl.when(me != target)
        def _():
            window_copy(slot, target).wait_send()

    @pl.when(is_worker)
    def _():
        @pl.loop(0, depth_count)
        def drain(layer):
            @pl.when(layer != me)
            def _():
                grad_copy(layer).wait_send()
                scale_copy(layer).wait_send()


def body(tables, object_slices, probe_wave, amplitudes, positions, counts):
    stripe = lax.axis_index("stripe")
    stripe_count = lax.axis_size("stripe")
    depth = lax.axis_index("depth")
    depth_count = lax.axis_size("depth")
    layers, _, stripe_rows, width = object_slices.shape
    length = probe_wave.shape[1]
    half = length // 2
    capacity = amplitudes.shape[0]
    stride = depth_count // capacity
    assert layers == 1 and stripe_rows == length and width == 3 * half and stride >= 2

    slab = jnp.round(object_slices[0] * LEVELS).astype(jnp.int16)
    back = [(i, (i + stripe_count - 1) % stripe_count) for i in range(stripe_count)]
    forth = [(i, (i + 1) % stripe_count) for i in range(stripe_count)]
    slab_next = lax.ppermute(slab, "stripe", back)

    mine = lax.dynamic_slice(positions, (stripe * capacity, 0), (capacity, 2)).astype(jnp.int32)
    rows, cols = mine[:, 0], mine[:, 1]
    live = (jnp.arange(capacity, dtype=jnp.int32) < counts[stripe]).astype(jnp.int32)
    here = jnp.arange(stripe_rows)[None, :] >= rows[:, None]
    near = jnp.arange(length)[None, :] >= cols[:, None]
    merged = jnp.where(here[:, None, :, None], slab[None], slab_next[None])
    folded = jnp.concatenate([merged[..., length:], merged[..., half:length]], axis=-1)
    windows = jnp.where(near[:, None, None, :], merged[..., :length], folded)

    my_slot = depth // stride
    row, col = rows[my_slot], cols[my_slot]
    doubled = jnp.concatenate([probe_wave, probe_wave], axis=1)
    probe = lax.dynamic_slice_in_dim(doubled, length - row, length, axis=1)
    doubled = jnp.concatenate([probe, probe], axis=2)
    probe = lax.dynamic_slice_in_dim(doubled, length - col, length, axis=2)
    amp = lax.dynamic_index_in_dim(amplitudes, my_slot, 0, keepdims=False)

    field = (2, length, length)
    vmem = pl.BlockSpec(memory_space=pltpu.VMEM)
    smem = pl.BlockSpec(memory_space=pltpu.SMEM)
    count = (tables.shape[0] - 2) // 4
    out = jax.ShapeDtypeStruct((2, stripe_rows, width), jnp.float32)
    own, following = pl.pallas_call(
        functools.partial(kernel, depth_count, capacity),
        out_shape=(out, out),
        in_specs=[smem] * 3 + [vmem] * 4,
        out_specs=(vmem, vmem),
        scratch_shapes=[
            pltpu.VMEM((depth_count,) + field, jnp.int16),
            pltpu.VMEM((depth_count,) + field, jnp.float32),
            pltpu.VMEM((depth_count,) + field, jnp.int16),
            pltpu.VMEM((depth_count, 8, length), jnp.float32),
            pltpu.VMEM((capacity,) + field, jnp.int16),
            pltpu.VMEM((capacity, 8, length), jnp.float32),
            pltpu.VMEM((count, 3 * length, length), jnp.bfloat16),
            pltpu.VMEM((count, length, 3 * length), jnp.bfloat16),
            pltpu.VMEM(field, jnp.float32),
            pltpu.SemaphoreType.DMA((capacity,)),
            pltpu.SemaphoreType.DMA((depth_count,)),
            pltpu.SemaphoreType.DMA((depth_count,)),
            pltpu.SemaphoreType.DMA((capacity,)),
            pltpu.SemaphoreType.DMA((depth_count,)),
            pltpu.SemaphoreType.DMA((capacity,)),
        ],
        compiler_params=pltpu.CompilerParams(
            collective_id=0, has_side_effects=True, vmem_limit_bytes=60 * 1024 * 1024
        ),
    )(rows, cols, live, windows, probe, amp, tables)
    received = lax.ppermute(following, "stripe", forth)
    return (own + received)[None]


def solution(mesh):
    def run(object_slices, probe_wave, amplitudes, positions, counts):
        tables = jnp.asarray(make_tables(probe_wave.shape[1]))
        return jax.shard_map(
            body,
            mesh=mesh,
            in_specs=(P(), P("depth", None, "stripe", None), P(), P("stripe", None, None), P(), P()),
            out_specs=P("depth", None, "stripe", None),
            check_vma=False,
        )(tables, object_slices, probe_wave, amplitudes, positions, counts)

    return run
```

time: 759 us -> 92.5 us (0.12)
  waiting for transfers between devices: 445 us -> 11.6 us
  local copies, waits for them, and re-layouts: 112 us -> 2.3 us
  starting transfers between devices: 102 us -> 2.55 us
  Pallas kernels: 0 us -> 63.8 us
  other arithmetic: 41.1 us -> 8.15 us
  loops' own time: 26.8 us -> 0 us
  matrix products: 16.8 us -> 0 us
  between operations: 13.2 us -> 3.84 us
    ppermute x18 -> x2, waiting for transfers between devices: 367 us -> 11.6 us  [the longest x1 11.6 us: body(): received = lax.ppermute(following, 'stripe', forth)]
    ppermute x18 -> x2, starting transfers between devices: 101 us -> 2.55 us  [the longest x1 2.49 us: body(): slab_next = lax.ppermute(slab, 'stripe', back)]
    pallas_call x0 -> x1, Pallas kernels: none -> 63.8 us  [body(): pl.pallas_call(functools.partial(kernel, depth_count, capacity), out_shap...]
    all_gather x2 -> x0, waiting for transfers between devices: 43.2 us -> none  [the longest x1 26.2 us: body(): whole_slab = lax.all_gather(object_slices, 'stripe', axis=2, tiled=True)]
    reduce_scatter x1 -> x0, waiting for transfers between devices: 34.6 us -> none  [body(): lax.psum_scatter(full_grad, 'stripe', scatter_dimension=2, tiled=True)]
    while x19 -> x0, local copies, waits for them, and re-layouts: 27.8 us -> none
    another operation x24 -> x0, loops' own time: 26.8 us -> none  [the longest x9 7.49 us: forward_step(): lax.cond(active, forward_compute_step, forward_skip_step, (stored, starts))]
    unnamed x8 -> x10, local copies, waits for them, and re-layouts: 19.7 us -> 0.02 us
  transfers between devices with their start and end apart: 21 -> 2, of which waited for: 21 -> 1; matrix products, arithmetic and copies ran while one was open for 4% -> 6% of each run, Pallas kernels for 0% -> 0%
where the time goes in v1:
time: 92.5 us; the launch traced here: 92.3 us
  Pallas kernels  63.8 us (69%)
  waiting for transfers between devices  11.6 us (13%)
  other arithmetic  8.15 us (9%)
  between operations  3.84 us (4%)
  starting transfers between devices  2.55 us (3%)
  local copies, waits for them, and re-layouts  2.3 us (2%)
    pallas_call x1, Pallas kernels, body(): pl.pallas_call(functools.partial(kernel, depth_count, capacity), out_shap...  63.8 us
    ppermute x1, waiting for transfers between devices, body(): received = lax.ppermute(following, 'stripe', forth)  11.6 us
    ppermute x1, starting transfers between devices, body(): slab_next = lax.ppermute(slab, 'stripe', back)  2.49 us
    broadcast_in_dim x1, other arithmetic, body(): return (own + received)[None]  2.09 us
  transfers between devices with their start and end apart: 2, of which 1 were waited for; matrix products, arithmetic and copies ran while one was open for 6% of the time, Pallas kernels for 0%

profile of v1, /device:TPU:0, one launch (start us, length us, event | category | flops | bytes accessed | tf_op | source)
XLA Modules:
  0.0 92.3 jit_solution(3677353446680903434)
XLA Ops:
  0.0 0.0 copy-start
  0.0 1.3 %fusion = s16[2,256,384]{2,1,0:T(8,128)(2,1)S(1)} fusion(f32[1,2,256,384]{3,2,1,0:T(8,128)} %param.6), kind=kLoop, calls=%fused_computation.8 | loop fusion | flops 589824 | bytes 1179648 | tf_op jit(solution)/shard_map/jit(_where)/broadcast_in_dim | solution.py:313
  1.3 2.5 %collective-permute-start = (s16[2,256,384]{2,1,0:T(8,128)(2,1)S(1)}, s16[2,256,384]{2,1,0:T(8,128)(2,1)S(1)}, u32[]{:S(2)}, u32[]{:S(2)}) collective-permute-start(s16[2,256,384]{2,1,0:T(8,128)(2,1)S(1)} %fusion), channel_id=1, source_target_pairs={{0,3},{1,0},{2,1},{3,2},{4,7},{5,4},{6,5},{7,6},{8,11},{9,8},{10,9... | collective-permute-start | bytes 1179656 | tf_op jit(solution)/shard_map/ppermute | solution.py:306
  3.8 0.7 constant_dynamic-slice_fusion.2
  4.6 0.7 fusion.5
  5.9 0.0 copy-done
  5.9 0.7 dynamic-slice_bitcast_fusion.amp_ref
  7.8 0.0 copy-done.1
  7.8 0.4 fusion.2
  8.2 0.0 copy-done.4
  8.2 0.6 dynamic_slice.23
  8.8 1.1 %compare_convert_fusion.live_ref = s32[4]{0:T(128)} fusion(s32[]{:T(128)} %bitcast.2), kind=kLoop, calls=%fused_computation.17 | loop fusion | flops 8 | bytes 20 | tf_op jit(solution)/shard_map/convert_element_type | solution.py:310
  11.8 1.0 %fusion.1.probe_ref = bf16[2,256,256]{2,1,0:T(8,128)(2,1)} fusion(s32[]{:T(128)S(6)} %select_n.38, bf16[2,256,256]{2,1,0:T(8,128)(2,1)S(1)} %fusion.2), kind=kLoop, calls=%fused_computation.9 | loop fusion | flops 524288 | bytes 524292 | tf_op jit(solution)/shard_map/concatenate | solution.py:321
  12.8 0.1 iota_compare_fusion
  12.8 0.0 collective-permute-done
  12.8 0.3 broadcast_select_fusion
  13.1 0.0 copy-done.2
  13.2 0.0 copy-done.3
  13.2 0.3 fusion.3
  13.4 1.2 %slice_select_fusion.win_ref = s16[4,2,256,256]{3,2,1,0:T(8,128)(2,1)} fusion(s16[4,2,256,384]{3,2,1,0:T(8,128)(2,1)S(1)} %broadcast_select_fusion, s16[4,2,256,128]{3,2,1,0:T(8,128)(2,1)S(1)} %get-tuple-element.10, s16[4,2,256,128]{3,2,1,0:T(8,128)(2,1)S(1)} %get-tuple-element.9, pred[4,256]{1,0:T(4,128)(4,1)S(1)} %get-tuple-element.20), kind=kLoop, calls=%fused_computation.1 | loop fusion | flops 1048576 | bytes 3146752 | tf_op jit(solution)/shard_map/jit(_where)/select_n | solution.py:315
  14.7 63.8 %shard_map.64 = (f32[2,256,384]{2,1,0:T(8,128)}, f32[2,256,384]{2,1,0:T(8,128)}) custom-call(s32[4]{0:T(128)} %copy-done.2, s32[4]{0:T(128)} %copy-done.3, s32[4]{0:T(128)} %compare_convert_fusion.live_ref, s16[4,2,256,256]{3,2,1,0:T(8,128)(2,1)} %slice_select_fusion.win_ref, bf16[2,256,256]{2,1,0:T(8,128)(2,1)} %fusion.1.probe_ref, ...), custom_call_target="tpu_custom_call" | custom-call | tf_op jit(solution)/shard_map/pallas_call | solution.py:330
  78.5 0.1 collective-permute-start.1
  78.6 11.6 %collective-permute-done.1 = f32[2,256,384]{2,1,0:T(8,128)S(1)} collective-permute-done((f32[2,256,384]{2,1,0:T(8,128)}, f32[2,256,384]{2,1,0:T(8,128)S(1)}, u32[]{:S(2)}, u32[]{:S(2)}) %collective-permute-start.1) | collective-permute-done | bytes 786464 | tf_op jit(solution)/shard_map/ppermute | solution.py:356
  90.2 2.1 %add_bitcast_fusion = f32[1,2,256,384]{3,2,1,0:T(8,128)} fusion(f32[2,256,384]{2,1,0:T(8,128)} %get-tuple-element.7, f32[2,256,384]{2,1,0:T(8,128)S(1)} %collective-permute-done.1), kind=kLoop, calls=%fused_computation.2 | loop fusion | flops 196608 | bytes 2359296 | tf_op jit(solution)/shard_map/broadcast_in_dim | solution.py:357
  (5 shorter events, 0.0 us)
Async XLA Ops:
  0.0 5.9 %copy-start = (bf16[4,256,256]{2,1,0:T(8,128)(2,1)S(1)}, bf16[4,256,256]{2,1,0:T(8,128)(2,1)}, u32[]{:S(2)}) copy-start(bf16[4,256,256]{2,1,0:T(8,128)(2,1)} %param.8) | copy-start | bytes 1572868
  0.0 7.8 %copy-start.1 = (bf16[2,256,256]{2,1,0:T(8,128)(2,1)S(1)}, bf16[2,256,256]{2,1,0:T(8,128)(2,1)}, u32[]{:S(2)}) copy-start(bf16[2,256,256]{2,1,0:T(8,128)(2,1)} %param.7) | copy-start | bytes 786436
  0.0 8.2 %copy-start.4 = (s32[4]{0:T(128)S(1)}, s32[4]{0:T(128)}, u32[]{:S(2)}) copy-start(s32[4]{0:T(128)} %param.10) | copy-start | bytes 52
  1.3 11.5 %collective-permute-start = (s16[2,256,384]{2,1,0:T(8,128)(2,1)S(1)}, s16[2,256,384]{2,1,0:T(8,128)(2,1)S(1)}, u32[]{:S(2)}, u32[]{:S(2)}) collective-permute-start(s16[2,256,384]{2,1,0:T(8,128)(2,1)S(1)} %fusion), channel_id=1, source_target_pairs={{0,3},{1,0},{2,1},{3,2},{4,7},{5,4},{6,5},{7,6},{8,11},{9,8},{10,9... | collective-permute-start | bytes 1179656 | tf_op jit(solution)/shard_map/ppermute | solution.py:306
  4.6 8.6 %copy-start.2 = (s32[4]{0:T(128)}, s32[4]{0:T(128)S(1)}, u32[]{:S(2)}) copy-start(s32[4]{0:T(128)S(1)} %get-tuple-element.12.rows_ref) | copy-start | bytes 52
  4.6 8.6 %copy-start.3 = (s32[4]{0:T(128)}, s32[4]{0:T(128)S(1)}, u32[]{:S(2)}) copy-start(s32[4]{0:T(128)S(1)} %get-tuple-element.13.cols_ref) | copy-start | bytes 52
  78.5 11.7 %collective-permute-start.1 = (f32[2,256,384]{2,1,0:T(8,128)}, f32[2,256,384]{2,1,0:T(8,128)S(1)}, u32[]{:S(2)}, u32[]{:S(2)}) collective-permute-start(f32[2,256,384]{2,1,0:T(8,128)} %get-tuple-element.8), channel_id=1, source_target_pairs={{0,1},{1,2},{2,3},{3,0},{4,5},{5,6},{6,7},{7,4},{8,9},{9,10},{10,1... | collective-permute-start | bytes 2359304 | tf_op jit(solution)/shard_map/ppermute | solution.py:356

commit v2 on v1

v2 whole, which is shorter than its diff:
```python
import functools

import jax
import jax.numpy as jnp
import numpy as np
from jax import lax
from jax.experimental import pallas as pl
from jax.experimental.pallas import tpu as pltpu
from jax.sharding import PartitionSpec as P

smoothing = 0.25
LEVELS = 32767.0
MESH = pl.DeviceIdType.MESH


def right_form(matrix):
    return np.block([[matrix.real, matrix.imag], [-matrix.imag, matrix.real]])


def make_tables(length):
    half = length // 2
    index = np.arange(length)
    dft = np.exp(-2j * np.pi * (np.outer(index, index) % length) / length) / np.sqrt(length)
    freq = (index + half) % length - half
    fresnel = np.exp(-1j * np.pi * freq.astype(np.float64) ** 2 / (2.0 * length))
    prop = dft.conj() @ (fresnel[:, None] * dft)
    first, second = prop[:half, :half], prop[:half, half:]
    parts = [(first + second) / 2, (first - second) / 2, dft[:half, 0::2], dft[:half, 1::2]]
    tables = []
    for part in parts:
        right = right_form(part)
        tables += [right, right.T]
    stacked = np.stack(tables).astype(np.float32)
    high = stacked.astype(jnp.bfloat16)
    low = (stacked - high.astype(np.float32)).astype(jnp.bfloat16)
    order = np.concatenate([np.arange(0, length, 2), np.arange(1, length, 2)])
    pick = np.zeros((length, length), np.float32)
    pick[np.arange(length), order] = 1.0
    picks = np.stack([pick, pick.T]).astype(jnp.bfloat16)
    return np.concatenate([high, low, picks], axis=0)


def parts_of(value):
    high = value.astype(jnp.bfloat16)
    low = (value - high.astype(jnp.float32)).astype(jnp.bfloat16)
    return high, low


def dot(a, b):
    return jnp.dot(a, b, preferred_element_type=jnp.float32)


def kernel(
    depth_count, stripe_count, capacity, positions_ref, counts_ref, object_ref, probe_ref, amp_ref,
    table_ref, out_ref,
    slab, slab_next, win, wins, waves, gout, gscale, gin, gin_scale, rstack, lstack, adj_buf,
    following, following_scale, given, given_scale,
    send_n, recv_n, send_w, recv_w, send_g, recv_g, send_s, recv_s, send_f, recv_f, send_fs, recv_fs,
):
    me = lax.axis_index("depth")
    stripe = lax.axis_index("stripe")
    stride = depth_count // capacity
    length = probe_ref.shape[-1]
    half = length // 2
    count = (table_ref.shape[0] - 2) // 2
    before = lax.rem(stripe + stripe_count - 1, stripe_count)
    after = lax.rem(stripe + 1, stripe_count)

    barrier = pltpu.get_barrier_semaphore()

    @pl.loop(1, depth_count)
    def greet(step):
        other = lax.rem(me + step, depth_count)
        pl.semaphore_signal(barrier, inc=1, device_id=(other, stripe), device_id_type=MESH)

    pl.semaphore_signal(barrier, inc=1, device_id=(me, before), device_id_type=MESH)
    pl.semaphore_signal(barrier, inc=1, device_id=(me, after), device_id_type=MESH)
    for part in range(2):
        slab[part] = jnp.round(object_ref[0, part] * LEVELS).astype(jnp.int32).astype(jnp.int16)
    pl.semaphore_wait(barrier, depth_count + 1)

    def slab_copy(part):
        return pltpu.make_async_remote_copy(
            src_ref=slab.at[part], dst_ref=slab_next.at[part], send_sem=send_n.at[part],
            recv_sem=recv_n.at[part], device_id=(me, before), device_id_type=MESH,
        )

    for part in range(2):
        slab_copy(part).start()

    def worker_of(slot):
        return slot * stride + lax.rem(slot + stripe, 2)

    my_slot = me // stride
    is_worker = me == worker_of(my_slot)

    @pl.when(is_worker)
    def _():
        for which in range(count // 2):
            high, low = table_ref[2 * which], table_ref[count + 2 * which]
            rstack[which] = jnp.concatenate([high, low, high], axis=0)
            high, low = table_ref[2 * which + 1], table_ref[count + 2 * which + 1]
            lstack[which] = jnp.concatenate([high, low, high], axis=1)
        gscale[...] = jnp.zeros(gscale.shape, jnp.float32)
        row = positions_ref[stripe * capacity + my_slot, 0]
        col = positions_ref[stripe * capacity + my_slot, 1]
        first = lax.broadcasted_iota(jnp.int32, (length, length), 0)
        second = lax.broadcasted_iota(jnp.int32, (length, length), 1)
        turned = second + row
        turned = jnp.where(turned >= length, turned - length, turned)
        turn_rows = jnp.where(first == turned, 1.0, 0.0).astype(jnp.bfloat16)
        turned = first + col
        turned = jnp.where(turned >= length, turned - length, turned)
        turn_cols = jnp.where(second == turned, 1.0, 0.0).astype(jnp.bfloat16)
        for part in range(2):
            value = dot(turn_rows, probe_ref[part]).astype(jnp.bfloat16)
            waves[0, part] = dot(value, turn_cols)

    def window_copy(slot, part, target):
        return pltpu.make_async_remote_copy(
            src_ref=win.at[slot, part], dst_ref=wins.at[me, part], send_sem=send_w.at[slot, part],
            recv_sem=recv_w.at[me, part], device_id=(target, stripe), device_id_type=MESH,
        )

    row_index = lax.broadcasted_iota(jnp.int32, (length, half), 0)
    col_index = lax.broadcasted_iota(jnp.int32, (length, half), 1)
    for part in range(2):
        slab_copy(part).wait_recv()
        for slot in range(capacity):
            row = positions_ref[stripe * capacity + slot, 0]
            col = positions_ref[stripe * capacity + slot, 1]
            here = row_index >= row
            near = col_index >= col
            left, mid, right = (
                jnp.where(
                    here,
                    slab[part, :, pl.ds(place * half, half)].astype(jnp.int32),
                    slab_next[part, :, pl.ds(place * half, half)].astype(jnp.int32),
                )
                for place in range(3)
            )
            win[slot, part, :, pl.ds(0, half)] = jnp.where(near, left, right).astype(jnp.int16)
            win[slot, part, :, pl.ds(half, half)] = mid.astype(jnp.int16)
            target = worker_of(slot)

            @pl.when(me != target)
            def _():
                window_copy(slot, part, target).start()

            @pl.when(me == target)
            def _():
                pltpu.make_async_copy(
                    win.at[slot, part], wins.at[me, part], recv_w.at[me, part]
                ).start()

    def wait_window(layer):
        for part in range(2):
            pltpu.make_async_copy(
                win.at[0, part], wins.at[layer, part], recv_w.at[layer, part]
            ).wait()

    def grad_copy(layer):
        return pltpu.make_async_remote_copy(
            src_ref=gout.at[layer], dst_ref=gin.at[my_slot], send_sem=send_g.at[layer],
            recv_sem=recv_g.at[my_slot], device_id=(layer, stripe), device_id_type=MESH,
        )

    def scale_copy(layer):
        return pltpu.make_async_remote_copy(
            src_ref=gscale.at[layer], dst_ref=gin_scale.at[my_slot], send_sem=send_s.at[layer],
            recv_sem=recv_s.at[my_slot], device_id=(layer, stripe), device_id_type=MESH,
        )

    def right_dot(value, which):
        high, low = parts_of(value)
        return dot(jnp.concatenate([high, high, low], axis=1), rstack[which])

    def left_dot(which, value):
        high, low = parts_of(value)
        return dot(lstack[which], jnp.concatenate([high, high, low], axis=0))

    def split_lanes(re, im):
        return (
            jnp.concatenate([re[:, :half] + re[:, half:], im[:, :half] + im[:, half:]], axis=1),
            jnp.concatenate([re[:, :half] - re[:, half:], im[:, :half] - im[:, half:]], axis=1),
        )

    def split_rows(re, im):
        return (
            jnp.concatenate([re[:half] + re[half:], im[:half] + im[half:]], axis=0),
            jnp.concatenate([re[:half] - re[half:], im[:half] - im[half:]], axis=0),
        )

    def join_lanes(p, q):
        return (
            jnp.concatenate([p[:, :half] + q[:, :half], p[:, :half] - q[:, :half]], axis=1),
            jnp.concatenate([p[:, half:] + q[:, half:], p[:, half:] - q[:, half:]], axis=1),
        )

    def join_rows(p, q):
        return (
            jnp.concatenate([p[:half] + q[:half], p[:half] - q[:half]], axis=0),
            jnp.concatenate([p[half:] + q[half:], p[half:] - q[half:]], axis=0),
        )

    def propagate(re, im):
        u, v = split_lanes(re, im)
        re, im = join_lanes(right_dot(u, 0), right_dot(v, 1))
        u, v = split_rows(re, im)
        return join_rows(left_dot(0, u), left_dot(1, v))

    def window_of(layer):
        value = wins[layer].astype(jnp.int32).astype(jnp.float32) * (1.0 / LEVELS)
        return value[0], value[1]

    def emit(layer, re, im):
        for part, value in enumerate((re, im)):
            most = jnp.max(jnp.abs(value), axis=0, keepdims=True)
            most = jnp.maximum(most, 1e-30)
            gout[layer, part] = jnp.round(value * (LEVELS / most)).astype(jnp.int32).astype(jnp.int16)
            gscale[layer, pl.ds(part, 1), :] = most * (1.0 / LEVELS)

        @pl.when(layer != me)
        def _():
            grad_copy(layer).start()
            scale_copy(layer).start()

        @pl.when(layer == me)
        def _():
            pltpu.make_async_copy(gout.at[layer], gin.at[my_slot], recv_g.at[my_slot]).start()
            pltpu.make_async_copy(gscale.at[layer], gin_scale.at[my_slot], recv_s.at[my_slot]).start()

    @pl.when(is_worker)
    def _():
        @pl.loop(0, depth_count - 1)
        def forward(layer):
            wait_window(layer)
            win_re, win_im = window_of(layer)
            re, im = waves[layer, 0], waves[layer, 1]
            re, im = propagate(re * win_re - im * win_im, re * win_im + im * win_re)
            waves[layer + 1, 0] = re
            waves[layer + 1, 1] = im

        last = depth_count - 1
        wait_window(last)
        win_re, win_im = window_of(last)
        wave_re, wave_im = waves[last, 0], waves[last, 1]
        re = wave_re * win_re - wave_im * win_im
        im = wave_re * win_im + wave_im * win_re
        u, v = split_lanes(re, im)
        even, odd = right_dot(u, 2), right_dot(v, 3)
        re = jnp.concatenate([even[:, :half], odd[:, :half]], axis=1)
        im = jnp.concatenate([even[:, half:], odd[:, half:]], axis=1)
        u, v = split_rows(re, im)
        even, odd = left_dot(2, u), left_dot(3, v)
        pick_rows, pick_cols = table_ref[2 * count], table_ref[2 * count + 1]
        amp = dot(dot(pick_rows, amp_ref[my_slot]).astype(jnp.bfloat16), pick_cols)
        re = jnp.concatenate([even[:half], odd[:half]], axis=0)
        im = jnp.concatenate([even[half:], odd[half:]], axis=0)
        factor = 1.0 - amp / jnp.sqrt(re * re + im * im + smoothing)
        re, im = factor * re, factor * im
        def left_back(which, value):
            high, low = parts_of(value)
            table = table_ref[2 * which]
            table_low = table_ref[count + 2 * which]
            return dot(table, high) + dot(table_low, high) + dot(table, low)

        def right_back(value, which):
            high, low = parts_of(value)
            table = table_ref[2 * which + 1]
            table_low = table_ref[count + 2 * which + 1]
            return dot(high, table) + dot(high, table_low) + dot(low, table)

        re, im = join_rows(
            left_back(2, jnp.concatenate([re[:half], im[:half]], axis=0)),
            left_back(3, jnp.concatenate([re[half:], im[half:]], axis=0)),
        )
        mid_re, mid_im = join_lanes(
            right_back(jnp.concatenate([re[:, :half], im[:, :half]], axis=1), 2),
            right_back(jnp.concatenate([re[:, half:], im[:, half:]], axis=1), 3),
        )
        emit(
            last,
            wave_re * mid_re + wave_im * mid_im,
            wave_re * mid_im - wave_im * mid_re,
        )
        adj_buf[0] = win_re * mid_re + win_im * mid_im
        adj_buf[1] = win_im * mid_re - win_re * mid_im

        @pl.loop(1, depth_count)
        def backward(step):
            layer = last - step
            mid_re, mid_conj = propagate(adj_buf[0], adj_buf[1])
            win_re, win_im = window_of(layer)
            wave_re, wave_im = waves[layer, 0], waves[layer, 1]
            emit(
                layer,
                wave_re * mid_re - wave_im * mid_conj,
                -(wave_re * mid_conj + wave_im * mid_re),
            )
            adj_buf[0] = win_re * mid_re - win_im * mid_conj
            adj_buf[1] = win_im * mid_re + win_re * mid_conj

    def following_copy(part):
        return pltpu.make_async_remote_copy(
            src_ref=following.at[part], dst_ref=given.at[part], send_sem=send_f.at[part],
            recv_sem=recv_f.at[part], device_id=(me, after), device_id_type=MESH,
        )

    def following_scale_copy(part):
        return pltpu.make_async_remote_copy(
            src_ref=following_scale.at[part], dst_ref=given_scale.at[part],
            send_sem=send_fs.at[part], recv_sem=recv_fs.at[part], device_id=(me, after),
            device_id_type=MESH,
        )

    following_scale[...] = jnp.zeros(following_scale.shape, jnp.float32)
    for slot in range(capacity):
        pltpu.make_async_copy(gout.at[0], gin.at[slot], recv_g.at[slot]).wait()
        pltpu.make_async_copy(gscale.at[0], gin_scale.at[slot], recv_s.at[slot]).wait()
    for part in range(2):
        own_sums, next_sums = [0.0] * 3, [0.0] * 3
        for slot in range(capacity):
            row = positions_ref[stripe * capacity + slot, 0]
            col = positions_ref[stripe * capacity + slot, 1]
            here = row_index >= row
            near = col_index >= col
            live = counts_ref[stripe] > slot
            scale = gin_scale[slot, pl.ds(part, 1), :]
            scale = jnp.where(live, scale, 0.0)
            left = gin[slot, part, :, pl.ds(0, half)].astype(jnp.int32).astype(jnp.float32)
            left = left * scale[:, :half]
            mid = gin[slot, part, :, pl.ds(half, half)].astype(jnp.int32).astype(jnp.float32)
            mid = mid * scale[:, half:]
            pieces = (jnp.where(near, left, 0.0), mid, jnp.where(near, 0.0, left))
            for place, piece in enumerate(pieces):
                own_sums[place] = own_sums[place] + jnp.where(here, piece, 0.0)
                next_sums[place] = next_sums[place] + jnp.where(here, 0.0, piece)
        for place in range(3):
            lanes = pl.ds(place * half, half)
            most = jnp.max(jnp.abs(next_sums[place]), axis=0, keepdims=True)
            most = jnp.maximum(most, 1e-30)
            whole = jnp.round(next_sums[place] * (LEVELS / most)).astype(jnp.int32)
            following[part, :, lanes] = whole.astype(jnp.int16)
            following_scale[part, pl.ds(0, 1), lanes] = most * (1.0 / LEVELS)
            out_ref[0, part, :, lanes] = own_sums[place]
        following_copy(part).start()
        following_scale_copy(part).start()

    for part in range(2):
        following_copy(part).wait_recv()
        following_scale_copy(part).wait_recv()
        value = given[part].astype(jnp.int32).astype(jnp.float32)
        out_ref[0, part] += value * given_scale[part, pl.ds(0, 1), :]

    for part in range(2):
        slab_copy(part).wait_send()
        following_copy(part).wait_send()
        following_scale_copy(part).wait_send()
    for slot in range(capacity):
        target = worker_of(slot)

        @pl.when(me != target)
        def _():
            for part in range(2):
                window_copy(slot, part, target).wait_send()

    @pl.when(is_worker)
    def _():
        @pl.loop(0, depth_count)
        def drain(layer):
            @pl.when(layer != me)
            def _():
                grad_copy(layer).wait_send()
                scale_copy(layer).wait_send()


def body(tables, object_slices, probe_wave, amplitudes, positions, counts):
    stripe_count = lax.axis_size("stripe")
    depth_count = lax.axis_size("depth")
    layers, _, stripe_rows, width = object_slices.shape
    length = probe_wave.shape[1]
    capacity = amplitudes.shape[0]
    assert layers == 1 and stripe_rows == length and 2 * width == 3 * length
    assert depth_count >= 2 * capacity and stripe_count > 2

    field = (2, length, length)
    slab = (2, stripe_rows, width)
    slab_scale = (2, 8, width)
    vmem = pl.BlockSpec(memory_space=pltpu.VMEM)
    smem = pl.BlockSpec(memory_space=pltpu.SMEM)
    dma = pltpu.SemaphoreType.DMA
    count = (tables.shape[0] - 2) // 4
    return pl.pallas_call(
        functools.partial(kernel, depth_count, stripe_count, capacity),
        out_shape=jax.ShapeDtypeStruct(object_slices.shape, jnp.float32),
        in_specs=[smem] * 2 + [vmem] * 4,
        out_specs=vmem,
        scratch_shapes=[
            pltpu.VMEM(slab, jnp.int16),
            pltpu.VMEM(slab, jnp.int16),
            pltpu.VMEM((capacity,) + field, jnp.int16),
            pltpu.VMEM((depth_count,) + field, jnp.int16),
            pltpu.VMEM((depth_count,) + field, jnp.float32),
            pltpu.VMEM((depth_count,) + field, jnp.int16),
            pltpu.VMEM((depth_count, 8, length), jnp.float32),
            pltpu.VMEM((capacity,) + field, jnp.int16),
            pltpu.VMEM((capacity, 8, length), jnp.float32),
            pltpu.VMEM((count, 3 * length, length), jnp.bfloat16),
            pltpu.VMEM((count, length, 3 * length), jnp.bfloat16),
            pltpu.VMEM(field, jnp.float32),
            pltpu.VMEM(slab, jnp.int16),
            pltpu.VMEM(slab_scale, jnp.float32),
            pltpu.VMEM(slab, jnp.int16),
            pltpu.VMEM(slab_scale, jnp.float32),
            dma((2,)),
            dma((2,)),
            dma((capacity, 2)),
            dma((depth_count, 2)),
            dma((depth_count,)),
            dma((capacity,)),
            dma((depth_count,)),
            dma((capacity,)),
            dma((2,)),
            dma((2,)),
            dma((2,)),
            dma((2,)),
        ],
        compiler_params=pltpu.CompilerParams(
            collective_id=0, has_side_effects=True, vmem_limit_bytes=60 * 1024 * 1024
        ),
    )(positions, counts, object_slices, probe_wave, amplitudes, tables)


def solution(mesh):
    def run(object_slices, probe_wave, amplitudes, positions, counts):
        tables = jnp.asarray(make_tables(probe_wave.shape[1]))
        return jax.shard_map(
            body,
            mesh=mesh,
            in_specs=(P(), P("depth", None, "stripe", None), P(), P("stripe", None, None), P(), P()),
            out_specs=P("depth", None, "stripe", None),
            check_vma=False,
        )(tables, object_slices, probe_wave, amplitudes, positions, counts)

    return run
```

time: 92.5 us -> 81.3 us (0.88)
  Pallas kernels: 63.8 us -> 77.7 us
  waiting for transfers between devices: 11.6 us -> 0 us
  other arithmetic: 8.15 us -> 0 us
  between operations: 3.84 us -> 0.01 us
  starting transfers between devices: 2.55 us -> 0 us
  local copies, waits for them, and re-layouts: 2.3 us -> 3.42 us
    pallas_call x1, Pallas kernels: 63.8 us -> 77.7 us  [body(): pl.pallas_call(functools.partial(kernel, depth_count, stripe_count, capac...]
    ppermute x2 -> x0, waiting for transfers between devices: 11.6 us -> none  [the longest x1 11.6 us: body(): received = lax.ppermute(following, 'stripe', forth)]
    broadcast_in_dim x2 -> x0, other arithmetic: 3.43 us -> none  [the longest x1 2.09 us: body(): return (own + received)[None]]
    unnamed x10 -> x2, local copies, waits for them, and re-layouts: 0.02 us -> 3.42 us
    ppermute x2 -> x0, starting transfers between devices: 2.55 us -> none  [the longest x1 2.49 us: body(): slab_next = lax.ppermute(slab, 'stripe', back)]
    select_n x2 -> x0, other arithmetic: 1.53 us -> none  [the longest x1 1.23 us: body(): windows = jnp.where(near[:, None, None, :], merged[..., :length], folded)]
    dynamic_slice x2 -> x0, local copies, waits for them, and re-layouts: 1.34 us -> none  [the longest x1 0.75 us: body(): lax.dynamic_slice(positions, (stripe * capacity, 0), (capacity, 2))]
    concatenate x2 -> x0, other arithmetic: 1.34 us -> none  [the longest x1 0.96 us: body(): doubled = jnp.concatenate([probe, probe], axis=2)]
  transfers between devices with their start and end apart: 2 -> 0, of which waited for: 1 -> 0; matrix products, arithmetic and copies ran while one was open for 6% -> 0% of each run, Pallas kernels for 0% -> 0%
where the time goes in v2:
time: 81.3 us; the launch traced here: 81.2 us
  Pallas kernels  77.7 us (96%)
  local copies, waits for them, and re-layouts  3.42 us (4%)
    pallas_call x1, Pallas kernels, body(): pl.pallas_call(functools.partial(kernel, depth_count, stripe_count, capac...  77.7 us
    unnamed x2, local copies, waits for them, and re-layouts  3.42 us

profile of v2, /device:TPU:0, one launch (start us, length us, event | category | flops | bytes accessed | tf_op | source)
XLA Modules:
  0.0 81.2 jit_solution(3869638953638363030)
XLA Ops:
  0.0 1.4 %copy.7.positions_ref = s32[16,2]{1,0:T(8,128)} copy(s32[16,2]{0,1:T(2,128)} %param.9) | data formatting | bytes 256 | tf_op args[3]
  1.4 77.7 %shard_map.64 = f32[1,2,256,384]{3,2,1,0:T(8,128)} custom-call(s32[16,2]{1,0:T(8,128)} %copy.7.positions_ref, s32[4]{0:T(128)} %counts_ref.1, f32[1,2,256,384]{3,2,1,0:T(8,128)} %object_ref.1, bf16[2,256,256]{2,1,0:T(8,128)(2,1)} %probe_ref.1, bf16[4,256,256]{2,1,0:T(8,128)(2,1)} %amp_ref.1, bf16[18,256,256]{2,1,0:T(8,128)(2,1)} %constant.2.clone.table_ref), custom_call_target="tpu_custom_call" | custom-call | tf_op jit(solution)/shard_map/pallas_call | solution.py:394
  79.1 2.1 %copy.9 = f32[1,2,256,384]{3,2,1,0:T(8,128)} copy(f32[1,2,256,384]{3,2,1,0:T(8,128)} %shard_map.64) | data formatting | bytes 1572864

commit v3 on v2

--- a/solution.py
+++ b/solution.py
@@ -53,18 +53,31 @@
 def kernel(
     depth_count, stripe_count, capacity, positions_ref, counts_ref, object_ref, probe_ref, amp_ref,
     table_ref, out_ref,
-    slab, slab_next, win, wins, waves, gout, gscale, gin, gin_scale, rstack, lstack, adj_buf,
-    following, following_scale, given, given_scale,
-    send_n, recv_n, send_w, recv_w, send_g, recv_g, send_s, recv_s, send_f, recv_f, send_fs, recv_fs,
+    slab_re, slab_im, win, wins, waves, gout, gscale, gin, gin_scale, rstack, lstack, adj_buf,
+    patterns, across, across_scale, given, given_scale,
+    send_n, recv_n, send_w, recv_w, send_g, recv_g, send_s, recv_s, send_h, send_hs, send_a, recv_a,
+    send_f, recv_f, send_fs, recv_fs,
 ):
     me = lax.axis_index("depth")
     stripe = lax.axis_index("stripe")
-    stride = depth_count // capacity
+    share = capacity // 2
+    stride = depth_count // (share + 2)
+    slabs = (slab_re, slab_im)
     length = probe_ref.shape[-1]
     half = length // 2
     count = (table_ref.shape[0] - 2) // 2
-    before = lax.rem(stripe + stripe_count - 1, stripe_count)
-    after = lax.rem(stripe + 1, stripe_count)
+    partner = stripe + 1 - 2 * lax.rem(stripe, 2)
+    opposite = lax.rem(stripe + 2, stripe_count)
+
+    def slot_of(place):
+        owner, passed, start = jnp.int32(0), jnp.int32(0), jnp.int32(0)
+        for other in range(1, stripe_count):
+            passed = passed + counts_ref[other - 1]
+            owner = owner + jnp.where(place >= passed, 1, 0)
+            start = jnp.where(place >= passed, passed, start)
+        within = jnp.clip(place - start, 0, capacity - 1)
+        slot = owner * capacity + within
+        return owner, within, positions_ref[slot, 0], positions_ref[slot, 1]
 
     barrier = pltpu.get_barrier_semaphore()
 
@@ -73,26 +86,56 @@
         other = lax.rem(me + step, depth_count)
         pl.semaphore_signal(barrier, inc=1, device_id=(other, stripe), device_id_type=MESH)
 
-    pl.semaphore_signal(barrier, inc=1, device_id=(me, before), device_id_type=MESH)
-    pl.semaphore_signal(barrier, inc=1, device_id=(me, after), device_id_type=MESH)
-    for part in range(2):
-        slab[part] = jnp.round(object_ref[0, part] * LEVELS).astype(jnp.int32).astype(jnp.int16)
-    pl.semaphore_wait(barrier, depth_count + 1)
-
-    def slab_copy(part):
-        return pltpu.make_async_remote_copy(
-            src_ref=slab.at[part], dst_ref=slab_next.at[part], send_sem=send_n.at[part],
-            recv_sem=recv_n.at[part], device_id=(me, before), device_id_type=MESH,
-        )
-
-    for part in range(2):
-        slab_copy(part).start()
+    for step in range(1, stripe_count):
+        other = lax.rem(stripe + step, stripe_count)
+        pl.semaphore_signal(barrier, inc=1, device_id=(me, other), device_id_type=MESH)
+    for part in range(2):
+        whole = jnp.round(object_ref[0, part] * LEVELS).astype(jnp.int32)
+        slabs[part][stripe] = whole.astype(jnp.int16)
+    pl.semaphore_wait(barrier, depth_count + stripe_count - 2)
+
+    def slab_copy(route, part):
+        source = opposite if route == 2 else stripe
+        target = opposite if route == 1 else partner
+        return pltpu.make_async_remote_copy(
+            src_ref=slabs[part].at[source], dst_ref=slabs[part].at[source],
+            send_sem=send_n.at[route, part], recv_sem=recv_n.at[route, part],
+            device_id=(me, target), device_id_type=MESH,
+        )
+
+    for part in range(2):
+        slab_copy(1, part).start()
+        slab_copy(0, part).start()
 
     def worker_of(slot):
-        return slot * stride + lax.rem(slot + stripe, 2)
-
-    my_slot = me // stride
+        return (slot + 1) * stride + lax.rem(stripe, 2)
+
+    base = jnp.maximum(me - lax.rem(stripe, 2), 0)
+    my_slot = jnp.clip(base // stride - 1, 0, share - 1)
     is_worker = me == worker_of(my_slot)
+    my_owner, my_within, my_row, my_col = slot_of(stripe * share + my_slot)
+
+    def pattern_copy(parity, turn):
+        return pltpu.make_async_remote_copy(
+            src_ref=amp_ref, dst_ref=patterns.at[stripe], send_sem=send_a.at[turn],
+            recv_sem=recv_a.at[stripe], device_id=(me, 2 * turn + parity), device_id_type=MESH,
+        )
+
+    def each_pattern_target(action):
+        for parity in range(2):
+            for slot in range(share):
+                for turn in range(stripe_count // 2):
+                    here = (me == (slot + 1) * stride + parity) & (stripe != 2 * turn + parity)
+
+                    @pl.when(here)
+                    def _():
+                        action(pattern_copy(parity, turn))
+
+    each_pattern_target(lambda copy: copy.start())
+
+    for part in range(2):
+        slab_copy(1, part).wait_recv()
+        slab_copy(2, part).start()
 
     @pl.when(is_worker)
     def _():
@@ -102,14 +145,13 @@
             high, low = table_ref[2 * which + 1], table_ref[count + 2 * which + 1]
             lstack[which] = jnp.concatenate([high, low, high], axis=1)
         gscale[...] = jnp.zeros(gscale.shape, jnp.float32)
-        row = positions_ref[stripe * capacity + my_slot, 0]
-        col = positions_ref[stripe * capacity + my_slot, 1]
+        pltpu.make_async_copy(amp_ref, patterns.at[stripe], recv_a.at[stripe]).start()
         first = lax.broadcasted_iota(jnp.int32, (length, length), 0)
         second = lax.broadcasted_iota(jnp.int32, (length, length), 1)
-        turned = second + row
+        turned = second + my_row
         turned = jnp.where(turned >= length, turned - length, turned)
         turn_rows = jnp.where(first == turned, 1.0, 0.0).astype(jnp.bfloat16)
-        turned = first + col
+        turned = first + my_col
         turned = jnp.where(turned >= length, turned - length, turned)
         turn_cols = jnp.where(second == turned, 1.0, 0.0).astype(jnp.bfloat16)
         for part in range(2):
@@ -125,17 +167,18 @@
     row_index = lax.broadcasted_iota(jnp.int32, (length, half), 0)
     col_index = lax.broadcasted_iota(jnp.int32, (length, half), 1)
     for part in range(2):
-        slab_copy(part).wait_recv()
-        for slot in range(capacity):
-            row = positions_ref[stripe * capacity + slot, 0]
-            col = positions_ref[stripe * capacity + slot, 1]
+        slab_copy(0, part).wait_recv()
+        slab_copy(2, part).wait_recv()
+        for slot in range(share):
+            owner, _, row, col = slot_of(stripe * share + slot)
+            later = lax.rem(owner + 1, stripe_count)
             here = row_index >= row
             near = col_index >= col
             left, mid, right = (
                 jnp.where(
                     here,
-                    slab[part, :, pl.ds(place * half, half)].astype(jnp.int32),
-                    slab_next[part, :, pl.ds(place * half, half)].astype(jnp.int32),
+                    slabs[part][owner, :, pl.ds(place * half, half)].astype(jnp.int32),
+                    slabs[part][later, :, pl.ds(place * half, half)].astype(jnp.int32),
                 )
                 for place in range(3)
             )
@@ -253,8 +296,10 @@
         im = jnp.concatenate([even[:, half:], odd[:, half:]], axis=1)
         u, v = split_rows(re, im)
         even, odd = left_dot(2, u), left_dot(3, v)
+        for source in range(stripe_count):
+            pltpu.make_async_copy(amp_ref, patterns.at[source], recv_a.at[source]).wait()
         pick_rows, pick_cols = table_ref[2 * count], table_ref[2 * count + 1]
-        amp = dot(dot(pick_rows, amp_ref[my_slot]).astype(jnp.bfloat16), pick_cols)
+        amp = dot(dot(pick_rows, patterns[my_owner, my_within]).astype(jnp.bfloat16), pick_cols)
         re = jnp.concatenate([even[:half], odd[:half]], axis=0)
         im = jnp.concatenate([even[half:], odd[half:]], axis=0)
         factor = 1.0 - amp / jnp.sqrt(re * re + im * im + smoothing)
@@ -301,63 +346,93 @@
             adj_buf[0] = win_re * mid_re - win_im * mid_conj
             adj_buf[1] = win_im * mid_re + win_re * mid_conj
 
-    def following_copy(part):
-        return pltpu.make_async_remote_copy(
-            src_ref=following.at[part], dst_ref=given.at[part], send_sem=send_f.at[part],
-            recv_sem=recv_f.at[part], device_id=(me, after), device_id_type=MESH,
-        )
-
-    def following_scale_copy(part):
-        return pltpu.make_async_remote_copy(
-            src_ref=following_scale.at[part], dst_ref=given_scale.at[part],
-            send_sem=send_fs.at[part], recv_sem=recv_fs.at[part], device_id=(me, after),
+    def across_copy(part):
+        return pltpu.make_async_remote_copy(
+            src_ref=across.at[part], dst_ref=given.at[part], send_sem=send_f.at[part],
+            recv_sem=recv_f.at[part], device_id=(me, opposite), device_id_type=MESH,
+        )
+
+    def across_scale_copy(part):
+        return pltpu.make_async_remote_copy(
+            src_ref=across_scale.at[part], dst_ref=given_scale.at[part],
+            send_sem=send_fs.at[part], recv_sem=recv_fs.at[part], device_id=(me, opposite),
             device_id_type=MESH,
         )
 
-    following_scale[...] = jnp.zeros(following_scale.shape, jnp.float32)
-    for slot in range(capacity):
+    def share_copy(slot):
+        return pltpu.make_async_remote_copy(
+            src_ref=gin.at[slot], dst_ref=gin.at[share + slot], send_sem=send_h.at[slot],
+            recv_sem=recv_g.at[share + slot], device_id=(me, partner), device_id_type=MESH,
+        )
+
+    def share_scale_copy(slot):
+        return pltpu.make_async_remote_copy(
+            src_ref=gin_scale.at[slot], dst_ref=gin_scale.at[share + slot],
+            send_sem=send_hs.at[slot], recv_sem=recv_s.at[share + slot],
+            device_id=(me, partner), device_id_type=MESH,
+        )
+
+    across_scale[...] = jnp.zeros(across_scale.shape, jnp.float32)
+    for slot in range(share):
         pltpu.make_async_copy(gout.at[0], gin.at[slot], recv_g.at[slot]).wait()
+        share_copy(slot).start()
         pltpu.make_async_copy(gscale.at[0], gin_scale.at[slot], recv_s.at[slot]).wait()
-    for part in range(2):
-        own_sums, next_sums = [0.0] * 3, [0.0] * 3
-        for slot in range(capacity):
-            row = positions_ref[stripe * capacity + slot, 0]
-            col = positions_ref[stripe * capacity + slot, 1]
+        share_scale_copy(slot).start()
+    for slot in range(share):
+        share_copy(slot).wait_recv()
+        share_scale_copy(slot).wait_recv()
+    places = [stripe * share + slot for slot in range(share)]
+    places += [partner * share + slot for slot in range(share)]
+    for part in range(2):
+        own_sums, far_sums = [0.0] * 3, [0.0] * 3
+        for slot in range(2 * share):
+            owner, _, row, col = slot_of(places[slot])
+            later = lax.rem(owner + 1, stripe_count)
             here = row_index >= row
             near = col_index >= col
-            live = counts_ref[stripe] > slot
             scale = gin_scale[slot, pl.ds(part, 1), :]
-            scale = jnp.where(live, scale, 0.0)
             left = gin[slot, part, :, pl.ds(0, half)].astype(jnp.int32).astype(jnp.float32)
             left = left * scale[:, :half]
             mid = gin[slot, part, :, pl.ds(half, half)].astype(jnp.int32).astype(jnp.float32)
             mid = mid * scale[:, half:]
             pieces = (jnp.where(near, left, 0.0), mid, jnp.where(near, 0.0, left))
+            gain = [
+                jnp.where(
+                    here,
+                    jnp.where(owner == target, 1.0, 0.0),
+                    jnp.where(later == target, 1.0, 0.0),
+                )
+                for target in (stripe, opposite)
+            ]
             for place, piece in enumerate(pieces):
-                own_sums[place] = own_sums[place] + jnp.where(here, piece, 0.0)
-                next_sums[place] = next_sums[place] + jnp.where(here, 0.0, piece)
+                own_sums[place] = own_sums[place] + piece * gain[0]
+                far_sums[place] = far_sums[place] + piece * gain[1]
         for place in range(3):
             lanes = pl.ds(place * half, half)
-            most = jnp.max(jnp.abs(next_sums[place]), axis=0, keepdims=True)
+            most = jnp.max(jnp.abs(far_sums[place]), axis=0, keepdims=True)
             most = jnp.maximum(most, 1e-30)
-            whole = jnp.round(next_sums[place] * (LEVELS / most)).astype(jnp.int32)
-            following[part, :, lanes] = whole.astype(jnp.int16)
-            following_scale[part, pl.ds(0, 1), lanes] = most * (1.0 / LEVELS)
+            whole = jnp.round(far_sums[place] * (LEVELS / most)).astype(jnp.int32)
+            across[part, :, lanes] = whole.astype(jnp.int16)
+            across_scale[part, pl.ds(0, 1), lanes] = most * (1.0 / LEVELS)
             out_ref[0, part, :, lanes] = own_sums[place]
-        following_copy(part).start()
-        following_scale_copy(part).start()
-
-    for part in range(2):
-        following_copy(part).wait_recv()
-        following_scale_copy(part).wait_recv()
+        across_copy(part).start()
+        across_scale_copy(part).start()
+
+    for part in range(2):
+        across_copy(part).wait_recv()
+        across_scale_copy(part).wait_recv()
         value = given[part].astype(jnp.int32).astype(jnp.float32)
         out_ref[0, part] += value * given_scale[part, pl.ds(0, 1), :]
 
     for part in range(2):
-        slab_copy(part).wait_send()
-        following_copy(part).wait_send()
-        following_scale_copy(part).wait_send()
-    for slot in range(capacity):
+        for route in range(3):
+            slab_copy(route, part).wait_send()
+        across_copy(part).wait_send()
+        across_scale_copy(part).wait_send()
+    each_pattern_target(lambda copy: copy.wait_send())
+    for slot in range(share):
+        share_copy(slot).wait_send()
+        share_scale_copy(slot).wait_send()
         target = worker_of(slot)
 
         @pl.when(me != target)
@@ -382,7 +457,8 @@
     length = probe_wave.shape[1]
     capacity = amplitudes.shape[0]
     assert layers == 1 and stripe_rows == length and 2 * width == 3 * length
-    assert depth_count >= 2 * capacity and stripe_count > 2
+    share = capacity // 2
+    assert depth_count >= 2 * (share + 2) and stripe_count == 4 and capacity % 2 == 0
 
     field = (2, length, length)
     slab = (2, stripe_rows, width)
@@ -397,30 +473,35 @@
         in_specs=[smem] * 2 + [vmem] * 4,
         out_specs=vmem,
         scratch_shapes=[
-            pltpu.VMEM(slab, jnp.int16),
-            pltpu.VMEM(slab, jnp.int16),
-            pltpu.VMEM((capacity,) + field, jnp.int16),
+            pltpu.VMEM((stripe_count, stripe_rows, width), jnp.int16),
+            pltpu.VMEM((stripe_count, stripe_rows, width), jnp.int16),
+            pltpu.VMEM((share,) + field, jnp.int16),
             pltpu.VMEM((depth_count,) + field, jnp.int16),
             pltpu.VMEM((depth_count,) + field, jnp.float32),
             pltpu.VMEM((depth_count,) + field, jnp.int16),
             pltpu.VMEM((depth_count, 8, length), jnp.float32),
-            pltpu.VMEM((capacity,) + field, jnp.int16),
-            pltpu.VMEM((capacity, 8, length), jnp.float32),
+            pltpu.VMEM((2 * share,) + field, jnp.int16),
+            pltpu.VMEM((2 * share, 8, length), jnp.float32),
             pltpu.VMEM((count, 3 * length, length), jnp.bfloat16),
             pltpu.VMEM((count, length, 3 * length), jnp.bfloat16),
             pltpu.VMEM(field, jnp.float32),
+            pltpu.VMEM((stripe_count,) + amplitudes.shape, amplitudes.dtype),
             pltpu.VMEM(slab, jnp.int16),
             pltpu.VMEM(slab_scale, jnp.float32),
             pltpu.VMEM(slab, jnp.int16),
             pltpu.VMEM(slab_scale, jnp.float32),
-            dma((2,)),
-            dma((2,)),
-            dma((capacity, 2)),
+            dma((3, 2)),
+            dma((3, 2)),
+            dma((share, 2)),
             dma((depth_count, 2)),
             dma((depth_count,)),
-            dma((capacity,)),
+            dma((2 * share,)),
             dma((depth_count,)),
-            dma((capacity,)),
+            dma((2 * share,)),
+            dma((share,)),
+            dma((share,)),
+            dma((stripe_count // 2,)),
+            dma((stripe_count,)),
             dma((2,)),
             dma((2,)),
             dma((2,)),

time: 81.3 us -> 74.2 us (0.913)
  Pallas kernels: 77.7 us -> 70.2 us
    pallas_call x1, Pallas kernels: 77.7 us -> 70.2 us  [body(): pl.pallas_call(functools.partial(kernel, depth_count, stripe_count, capac...]
where the time goes in v3:
time: 74.2 us; the launch traced here: 73.6 us
  Pallas kernels  70.2 us (95%)
  local copies, waits for them, and re-layouts  3.42 us (5%)
    pallas_call x1, Pallas kernels, body(): pl.pallas_call(functools.partial(kernel, depth_count, stripe_count, capac...  70.2 us
    unnamed x2, local copies, waits for them, and re-layouts  3.42 us

profile of v3, /device:TPU:0, one launch (start us, length us, event | category | flops | bytes accessed | tf_op | source)
XLA Modules:
  0.0 73.6 jit_solution(10868894769859481043)
XLA Ops:
  0.0 1.4 %copy.7.positions_ref = s32[16,2]{1,0:T(8,128)} copy(s32[16,2]{0,1:T(2,128)} %param.9) | data formatting | bytes 256 | tf_op args[3]
  1.4 70.2 %shard_map.64 = f32[1,2,256,384]{3,2,1,0:T(8,128)} custom-call(s32[16,2]{1,0:T(8,128)} %copy.7.positions_ref, s32[4]{0:T(128)} %counts_ref.1, f32[1,2,256,384]{3,2,1,0:T(8,128)} %object_ref.1, bf16[2,256,256]{2,1,0:T(8,128)(2,1)} %probe_ref.1, bf16[4,256,256]{2,1,0:T(8,128)(2,1)} %amp_ref.1, bf16[18,256,256]{2,1,0:T(8,128)(2,1)} %constant.2.clone.table_ref), custom_call_target="tpu_custom_call" | custom-call | tf_op jit(solution)/shard_map/pallas_call | solution.py:470
  71.5 2.1 %copy.9 = f32[1,2,256,384]{3,2,1,0:T(8,128)} copy(f32[1,2,256,384]{3,2,1,0:T(8,128)} %shard_map.64) | data formatting | bytes 1572864

commit v4 on v3

--- a/solution.py
+++ b/solution.py
@@ -52,9 +52,9 @@
 
 def kernel(
     depth_count, stripe_count, capacity, positions_ref, counts_ref, object_ref, probe_ref, amp_ref,
-    table_ref, out_ref,
+    table_hbm, out_ref,
     slab_re, slab_im, win, wins, waves, gout, gscale, gin, gin_scale, rstack, lstack, adj_buf,
-    patterns, across, across_scale, given, given_scale,
+    table_ref, table_sem, patterns, across, across_scale, given, given_scale,
     send_n, recv_n, send_w, recv_w, send_g, recv_g, send_s, recv_s, send_h, send_hs, send_a, recv_a,
     send_f, recv_f, send_fs, recv_fs,
 ):
@@ -77,7 +77,15 @@
             start = jnp.where(place >= passed, passed, start)
         within = jnp.clip(place - start, 0, capacity - 1)
         slot = owner * capacity + within
-        return owner, within, positions_ref[slot, 0], positions_ref[slot, 1]
+        return owner, within, positions_ref[0, slot], positions_ref[1, slot]
+
+    share_base = jnp.maximum(me - lax.rem(stripe, 2), 0)
+    my_slot = jnp.clip(share_base // stride - 1, 0, share - 1)
+    is_worker = me == (my_slot + 1) * stride + lax.rem(stripe, 2)
+
+    @pl.when(is_worker)
+    def _():
+        pltpu.make_async_copy(table_hbm, table_ref, table_sem).start()
 
     barrier = pltpu.get_barrier_semaphore()
 
@@ -110,9 +118,6 @@
     def worker_of(slot):
         return (slot + 1) * stride + lax.rem(stripe, 2)
 
-    base = jnp.maximum(me - lax.rem(stripe, 2), 0)
-    my_slot = jnp.clip(base // stride - 1, 0, share - 1)
-    is_worker = me == worker_of(my_slot)
     my_owner, my_within, my_row, my_col = slot_of(stripe * share + my_slot)
 
     def pattern_copy(parity, turn):
@@ -139,6 +144,7 @@
 
     @pl.when(is_worker)
     def _():
+        pltpu.make_async_copy(table_hbm, table_ref, table_sem).wait()
         for which in range(count // 2):
             high, low = table_ref[2 * which], table_ref[count + 2 * which]
             rstack[which] = jnp.concatenate([high, low, high], axis=0)
@@ -202,16 +208,16 @@
                 win.at[0, part], wins.at[layer, part], recv_w.at[layer, part]
             ).wait()
 
-    def grad_copy(layer):
-        return pltpu.make_async_remote_copy(
-            src_ref=gout.at[layer], dst_ref=gin.at[my_slot], send_sem=send_g.at[layer],
-            recv_sem=recv_g.at[my_slot], device_id=(layer, stripe), device_id_type=MESH,
-        )
-
-    def scale_copy(layer):
-        return pltpu.make_async_remote_copy(
-            src_ref=gscale.at[layer], dst_ref=gin_scale.at[my_slot], send_sem=send_s.at[layer],
-            recv_sem=recv_s.at[my_slot], device_id=(layer, stripe), device_id_type=MESH,
+    def grad_copy(layer, part):
+        return pltpu.make_async_remote_copy(
+            src_ref=gout.at[layer, part], dst_ref=gin.at[my_slot, part],
+            send_sem=send_g.at[layer, part], recv_sem=recv_g.at[my_slot, part], device_id=(layer, stripe), device_id_type=MESH,
+        )
+
+    def scale_copy(layer, part):
+        return pltpu.make_async_remote_copy(
+            src_ref=gscale.at[layer, part], dst_ref=gin_scale.at[my_slot, part],
+            send_sem=send_s.at[layer, part], recv_sem=recv_s.at[my_slot, part], device_id=(layer, stripe), device_id_type=MESH,
         )
 
     def right_dot(value, which):
@@ -261,17 +267,21 @@
             most = jnp.max(jnp.abs(value), axis=0, keepdims=True)
             most = jnp.maximum(most, 1e-30)
             gout[layer, part] = jnp.round(value * (LEVELS / most)).astype(jnp.int32).astype(jnp.int16)
-            gscale[layer, pl.ds(part, 1), :] = most * (1.0 / LEVELS)
-
-        @pl.when(layer != me)
-        def _():
-            grad_copy(layer).start()
-            scale_copy(layer).start()
-
-        @pl.when(layer == me)
-        def _():
-            pltpu.make_async_copy(gout.at[layer], gin.at[my_slot], recv_g.at[my_slot]).start()
-            pltpu.make_async_copy(gscale.at[layer], gin_scale.at[my_slot], recv_s.at[my_slot]).start()
+            gscale[layer, part, pl.ds(0, 1), :] = most * (1.0 / LEVELS)
+
+            @pl.when(layer != me)
+            def _():
+                grad_copy(layer, part).start()
+                scale_copy(layer, part).start()
+
+            @pl.when(layer == me)
+            def _():
+                pltpu.make_async_copy(
+                    gout.at[layer, part], gin.at[my_slot, part], recv_g.at[my_slot, part]
+                ).start()
+                pltpu.make_async_copy(
+                    gscale.at[layer, part], gin_scale.at[my_slot, part], recv_s.at[my_slot, part]
+                ).start()
 
     @pl.when(is_worker)
     def _():
@@ -359,38 +369,43 @@
             device_id_type=MESH,
         )
 
-    def share_copy(slot):
-        return pltpu.make_async_remote_copy(
-            src_ref=gin.at[slot], dst_ref=gin.at[share + slot], send_sem=send_h.at[slot],
-            recv_sem=recv_g.at[share + slot], device_id=(me, partner), device_id_type=MESH,
-        )
-
-    def share_scale_copy(slot):
-        return pltpu.make_async_remote_copy(
-            src_ref=gin_scale.at[slot], dst_ref=gin_scale.at[share + slot],
-            send_sem=send_hs.at[slot], recv_sem=recv_s.at[share + slot],
+    def share_copy(slot, part):
+        return pltpu.make_async_remote_copy(
+            src_ref=gin.at[slot, part], dst_ref=gin.at[share + slot, part],
+            send_sem=send_h.at[slot, part], recv_sem=recv_g.at[share + slot, part],
             device_id=(me, partner), device_id_type=MESH,
         )
 
+    def share_scale_copy(slot, part):
+        return pltpu.make_async_remote_copy(
+            src_ref=gin_scale.at[slot, part], dst_ref=gin_scale.at[share + slot, part],
+            send_sem=send_hs.at[slot, part], recv_sem=recv_s.at[share + slot, part],
+            device_id=(me, partner), device_id_type=MESH,
+        )
+
     across_scale[...] = jnp.zeros(across_scale.shape, jnp.float32)
-    for slot in range(share):
-        pltpu.make_async_copy(gout.at[0], gin.at[slot], recv_g.at[slot]).wait()
-        share_copy(slot).start()
-        pltpu.make_async_copy(gscale.at[0], gin_scale.at[slot], recv_s.at[slot]).wait()
-        share_scale_copy(slot).start()
-    for slot in range(share):
-        share_copy(slot).wait_recv()
-        share_scale_copy(slot).wait_recv()
     places = [stripe * share + slot for slot in range(share)]
     places += [partner * share + slot for slot in range(share)]
     for part in range(2):
+        for slot in range(share):
+            pltpu.make_async_copy(
+                gout.at[0, part], gin.at[slot, part], recv_g.at[slot, part]
+            ).wait()
+            share_copy(slot, part).start()
+            pltpu.make_async_copy(
+                gscale.at[0, part], gin_scale.at[slot, part], recv_s.at[slot, part]
+            ).wait()
+            share_scale_copy(slot, part).start()
+        for slot in range(share):
+            share_copy(slot, part).wait_recv()
+            share_scale_copy(slot, part).wait_recv()
         own_sums, far_sums = [0.0] * 3, [0.0] * 3
         for slot in range(2 * share):
             owner, _, row, col = slot_of(places[slot])
             later = lax.rem(owner + 1, stripe_count)
             here = row_index >= row
             near = col_index >= col
-            scale = gin_scale[slot, pl.ds(part, 1), :]
+            scale = gin_scale[slot, part, pl.ds(0, 1), :]
             left = gin[slot, part, :, pl.ds(0, half)].astype(jnp.int32).astype(jnp.float32)
             left = left * scale[:, :half]
             mid = gin[slot, part, :, pl.ds(half, half)].astype(jnp.int32).astype(jnp.float32)
@@ -431,8 +446,9 @@
         across_scale_copy(part).wait_send()
     each_pattern_target(lambda copy: copy.wait_send())
     for slot in range(share):
-        share_copy(slot).wait_send()
-        share_scale_copy(slot).wait_send()
+        for part in range(2):
+            share_copy(slot, part).wait_send()
+            share_scale_copy(slot, part).wait_send()
         target = worker_of(slot)
 
         @pl.when(me != target)
@@ -446,8 +462,9 @@
         def drain(layer):
             @pl.when(layer != me)
             def _():
-                grad_copy(layer).wait_send()
-                scale_copy(layer).wait_send()
+                for part in range(2):
+                    grad_copy(layer, part).wait_send()
+                    scale_copy(layer, part).wait_send()
 
 
 def body(tables, object_slices, probe_wave, amplitudes, positions, counts):
@@ -470,7 +487,7 @@
     return pl.pallas_call(
         functools.partial(kernel, depth_count, stripe_count, capacity),
         out_shape=jax.ShapeDtypeStruct(object_slices.shape, jnp.float32),
-        in_specs=[smem] * 2 + [vmem] * 4,
+        in_specs=[smem] * 2 + [vmem] * 3 + [pl.BlockSpec(memory_space=pl.ANY)],
         out_specs=vmem,
         scratch_shapes=[
             pltpu.VMEM((stripe_count, stripe_rows, width), jnp.int16),
@@ -479,12 +496,14 @@
             pltpu.VMEM((depth_count,) + field, jnp.int16),
             pltpu.VMEM((depth_count,) + field, jnp.float32),
             pltpu.VMEM((depth_count,) + field, jnp.int16),
-            pltpu.VMEM((depth_count, 8, length), jnp.float32),
+            pltpu.VMEM((depth_count, 2, 8, length), jnp.float32),
             pltpu.VMEM((2 * share,) + field, jnp.int16),
-            pltpu.VMEM((2 * share, 8, length), jnp.float32),
+            pltpu.VMEM((2 * share, 2, 8, length), jnp.float32),
             pltpu.VMEM((count, 3 * length, length), jnp.bfloat16),
             pltpu.VMEM((count, length, 3 * length), jnp.bfloat16),
             pltpu.VMEM(field, jnp.float32),
+            pltpu.VMEM(tables.shape, tables.dtype),
+            dma,
             pltpu.VMEM((stripe_count,) + amplitudes.shape, amplitudes.dtype),
             pltpu.VMEM(slab, jnp.int16),
             pltpu.VMEM(slab_scale, jnp.float32),
@@ -494,12 +513,12 @@
             dma((3, 2)),
             dma((share, 2)),
             dma((depth_count, 2)),
-            dma((depth_count,)),
-            dma((2 * share,)),
-            dma((depth_count,)),
-            dma((2 * share,)),
-            dma((share,)),
-            dma((share,)),
+            dma((depth_count, 2)),
+            dma((2 * share, 2)),
+            dma((depth_count, 2)),
+            dma((2 * share, 2)),
+            dma((share, 2)),
+            dma((share, 2)),
             dma((stripe_count // 2,)),
             dma((stripe_count,)),
             dma((2,)),
@@ -510,7 +529,7 @@
         compiler_params=pltpu.CompilerParams(
             collective_id=0, has_side_effects=True, vmem_limit_bytes=60 * 1024 * 1024
         ),
-    )(positions, counts, object_slices, probe_wave, amplitudes, tables)
+    )(positions.T, counts, object_slices, probe_wave, amplitudes, tables)
 
 
 def solution(mesh):

time: 74.2 us -> 71.6 us (0.965)
  local copies, waits for them, and re-layouts: 3.42 us -> 2.06 us
  Pallas kernels: 70.2 us -> 69.4 us
    unnamed x2 -> x1, local copies, waits for them, and re-layouts: 3.42 us -> 2.06 us
    pallas_call x1, Pallas kernels: 70.2 us -> 69.4 us  [body(): pl.pallas_call(functools.partial(kernel, depth_count, stripe_count, capac...]
where the time goes in v4:
time: 71.6 us; the launch traced here: 71.5 us
  Pallas kernels  69.4 us (97%)
  local copies, waits for them, and re-layouts  2.06 us (3%)
    pallas_call x1, Pallas kernels, body(): pl.pallas_call(functools.partial(kernel, depth_count, stripe_count, capac...  69.4 us
    unnamed x1, local copies, waits for them, and re-layouts  2.06 us

profile of v4, /device:TPU:0, one launch (start us, length us, event | category | flops | bytes accessed | tf_op | source)
XLA Modules:
  0.0 71.5 jit_solution(6111680962756873196)
XLA Ops:
  0.0 69.4 %shard_map.64 = f32[1,2,256,384]{3,2,1,0:T(8,128)} custom-call(s32[2,16]{1,0:T(2,128)} %bitcast.1, s32[4]{0:T(128)} %counts_ref.1, f32[1,2,256,384]{3,2,1,0:T(8,128)} %object_ref.1, bf16[2,256,256]{2,1,0:T(8,128)(2,1)} %probe_ref.1, bf16[4,256,256]{2,1,0:T(8,128)(2,1)} %amp_ref.1, bf16[18,256,256]{2,1,0:T(8,128)(2,1)} %constant.2.clone.table_hbm), custom_call_target="tpu_custom_call" | custom-call | tf_op jit(solution)/shard_map/pallas_call | solution.py:487
  69.4 2.1 %copy.8 = f32[1,2,256,384]{3,2,1,0:T(8,128)} copy(f32[1,2,256,384]{3,2,1,0:T(8,128)} %shard_map.64) | data formatting | bytes 1572864
